TPU v7x, 512 devices: a whole 4x8x8 slice. The times are simulated.
512 devices in a mesh: tm: 128 (over y, z, core), sy: 2 (over x_lo), sx: 2 (over x_hi).
Axes of the slice: x: 4 (x_hi: 2, x_lo: 2; x = x_hi * 2 + x_lo), y: 8, z: 8, core: 2. Of those that a mesh axis runs over, the one named last changes fastest.
Arguments:
- frames: bfloat16 [512, 32, 32, 256], P('tm', 'sy', 'sx'), may hold values from -6 to 6
- in_kernel: bfloat16 [5, 5, 256, 128], replicated, may hold values from -0.078125 to 0.078125
- dt_weight: bfloat16 [256], replicated, may hold values from -1 to 1
- rates: float32 [128], replicated
- out_kernel: bfloat16 [3, 3, 128, 256], replicated, may hold values from -0.1875 to 0.1875
- skip: float32 [256], replicated, may hold values from 0.1 to 1.9
Outputs:
- output: bfloat16 [512, 32, 32, 256], P('tm', 'sy', 'sx')
All inputs are finite; a program needn't handle non-finite values.
Results may differ from a plain program's by a relative error of at most 0.001.
Values may be sent and summed in bfloat16 or wider, within the bound.
A program may use at most 128 MiB of HBM per device.

v0:
```python
import jax
import jax.numpy as jnp
from jax import lax
from jax.sharding import PartitionSpec as P


def with_halo(block, sides, width):
    for axis, dim in sides:
        count = lax.axis_size(axis)
        forward = [(i, i + 1) for i in range(count - 1)]
        backward = [(target, source) for source, target in forward]
        low = lax.ppermute(
            lax.slice_in_dim(block, block.shape[dim] - width, None, axis=dim), axis, forward
        )
        high = lax.ppermute(lax.slice_in_dim(block, 0, width, axis=dim), axis, backward)
        block = jnp.concatenate([low, block, high], axis=dim)
    return block


def prefix(value, axis, combine, identity):
    length, index = (lax.axis_size(axis), lax.axis_index(axis))
    everything = jax.tree.map(lambda part: lax.all_gather(part, axis), value)
    start = jax.tree.map(
        lambda part, zero: jnp.broadcast_to(jnp.asarray(zero, part.dtype), part.shape),
        value,
        identity,
    )

    def step(k, before):
        reached = k < index
        new = combine(before, jax.tree.map(lambda part: part[k], everything))
        return jax.tree.map(lambda a, b: jnp.where(reached, a, b), new, before)

    return lax.fori_loop(0, length, step, start)


def convolve(padded, kernel):
    return lax.conv_general_dilated(
        padded,
        kernel,
        (1, 1),
        "VALID",
        dimension_numbers=("NHWC", "HWIO", "NHWC"),
        preferred_element_type=jnp.float32,
    )


def convolve_exact(padded, kernel):
    return lax.conv_general_dilated(
        padded,
        kernel.astype(jnp.float32),
        (1, 1),
        "VALID",
        dimension_numbers=("NHWC", "HWIO", "NHWC"),
        precision=lax.Precision.HIGHEST,
        preferred_element_type=jnp.float32,
    )


def body(frames, in_kernel, dt_weight, rates, out_kernel, skip):
    widened = with_halo(frames, (("sy", 1), ("sx", 2)), 2)
    drive = convolve(widened, in_kernel)
    step = jax.nn.softplus(jnp.dot(frames, dt_weight, preferred_element_type=jnp.float32))
    count = frames.shape[0]
    state = jnp.zeros(drive.shape[1:], jnp.float32)
    summed = jnp.zeros(step.shape[1:], jnp.float32)
    locals_list = []
    summed_list = []
    for frame in range(count):
        scaled = step[frame][..., None] * rates
        state = jnp.exp(-scaled) * state + jnp.sqrt(-jnp.expm1(-2.0 * scaled)) * drive[frame]
        summed = summed + step[frame]
        locals_list.append(state)
        summed_list.append(summed)

    def compose(earlier, later):
        return (earlier[0] * later[0], later[0] * earlier[1] + later[1])

    product = jnp.exp(-summed[..., None] * rates)
    identity = (jnp.ones_like(product), jnp.zeros_like(state))
    _, incoming = prefix((product, state), "tm", compose, identity)
    hidden_list = []
    for frame in range(count):
        fixed = locals_list[frame] + jnp.exp(-summed_list[frame][..., None] * rates) * incoming
        hidden_list.append(fixed)
    hidden = jnp.stack(hidden_list, axis=0)
    rimmed = with_halo(hidden, (("sy", 1), ("sx", 2)), 1)
    mixed = convolve_exact(rimmed, out_kernel) + skip * frames.astype(jnp.float32)
    return mixed.astype(jnp.bfloat16)


def solution(mesh):
    return jax.shard_map(
        body,
        mesh=mesh,
        in_specs=(P("tm", "sy", "sx", None), P(), P(), P(), P(), P()),
        out_specs=P("tm", "sy", "sx", None),
        check_vma=False,
    )
```

profile of v0, /device:TPU:57, one launch (start us, length us, event | category | flops | bytes accessed | tf_op | source)
XLA Modules:
  0.0 412.9 jit_solution(17111293760634097371)
XLA Ops:
  7.6 3.1 collective-permute-start
  10.8 1.3 collective-permute-start.1
  12.8 1.7 fusion.73
  15.9 4.4 %collective-permute-start.2 = (bf16[4,20,2,256]{3,0,2,1:T(4,128)(2,1)S(1)}, bf16[4,20,2,256]{3,0,2,1:T(4,128)(2,1)S(1)}, u32[]{:S(2)}, u32[]{:S(2)}) collective-permute-start(bf16[4,20,2,256]{3,0,2,1:T(4,128)(2,1)S(1)} %get-tuple-element.130), channel_id=1, source_target_pairs={{0,1},{2,3},{4,5},{6,7},{8,9},{10,11},{12,13},{14,15},{16,17},{18,... | collective-permute-start | bytes 245768 | tf_op jit(solution)/shard_map/ppermute | solution.py:12
  20.3 1.3 collective-permute-start.3
  21.8 5.2 %collective-permute-done.3 = bf16[4,20,2,256]{3,0,2,1:T(4,128)(2,1)S(1)} collective-permute-done((bf16[4,20,2,256]{3,0,2,1:T(4,128)(2,1)S(1)}, bf16[4,20,2,256]{3,0,2,1:T(4,128)(2,1)S(1)}, u32[]{:S(2)}, u32[]{:S(2)}) %collective-permute-start.3) | collective-permute-done | bytes 81952 | tf_op jit(solution)/shard_map/ppermute | solution.py:15
  27.0 5.0 %fusion.9 = f32[4,16,16,128]{3,0,2,1:T(4,128)S(1)} fusion(bf16[5,5,256,128]{3,2,1,0:T(8,128)(2,1)S(1)} %copy-done, bf16[4,20,2,256]{3,0,2,1:T(4,128)(2,1)S(1)} %collective-permute-done.3, bf16[4,20,16,256]{3,0,2,1:T(4,128)(2,1)S(1)} %constant_dynamic-update-slice_fusion, bf16[4,20,2,256]{3,0,2,1:T(4,128)(2,1)S(1)} %collective-permute-done.2), kind=kOutput, calls=%fused_computation.13 | convolution fusion | flops 1680179200 | bytes 2981888 | tf_op jit(solution)/shard_map/conv_general_dilated | solution.py:38
  32.4 1.2 fusion.24
  34.3 104.4 %all-gather.3.cloned.1.call-done = f32[128,16,16,128]{3,2,1,0:T(8,128)} async-done(((f32[1,16,16,128]{3,2,1,0:T(8,128)}), f32[128,16,16,128]{3,2,1,0:T(8,128)}) %all-gather.3.cloned.1.call-update) | async-done | bytes 16777232 | tf_op jit(solution)/shard_map/all_gather | solution.py:22
  138.7 101.3 %all-gather.5.cloned.1.call-done = f32[128,16,16,128]{3,2,1,0:T(8,128)} async-done(((f32[1,16,16,128]{3,2,1,0:T(8,128)}), f32[128,16,16,128]{3,2,1,0:T(8,128)}) %all-gather.5.cloned.1.call-update) | async-done | bytes 16777232 | tf_op jit(solution)/shard_map/all_gather | solution.py:22
  240.0 139.9 %while.14 = (s32[]{:T(128)}, f32[16,16,128]{2,1,0:T(8,128)S(1)}, s32[]{:T(128)}, f32[128,16,16,128]{3,2,1,0:T(8,128)}, f32[128,16,16,128]{3,2,1,0:T(8,128)}, /*index=5*/s32[]{:T(128)}, s32[]{:T(128)}) while((s32[]{:T(128)}, f32[16,16,128]{2,1,0:T(8,128)S(1)}, s32[]{:T(128)}, f32[128,16,16,128]{3,2,1,0:T(8,128)}, ...), condition=%wide.region_1.2_spmd.clone, body=%wide.region_0.1_spmd.clone.sunk | while | flops 131076 | bytes 524389 | solution.py:34
  241.1 1.1 fusion.87
  242.2 1.1 fusion.87
  243.3 1.1 fusion.87
  244.4 1.1 fusion.87
  245.5 1.1 fusion.87
  249.9 1.1 fusion.87
  380.6 3.1 collective-permute-start.4
  383.7 1.3 collective-permute-start.5
  385.0 3.3 collective-permute-done.5
  388.4 4.3 %collective-permute-start.6 = (f32[4,18,1,128]{3,2,1,0:T(1,128)S(1)}, f32[4,18,1,128]{3,2,1,0:T(1,128)S(1)}, u32[]{:S(2)}, u32[]{:S(2)}) collective-permute-start(f32[4,18,1,128]{3,2,1,0:T(1,128)S(1)} %get-tuple-element.132), channel_id=1, source_target_pairs={{0,1},{2,3},{4,5},{6,7},{8,9},{10,11},{12,13},{14,15},{16,17},{18,... | collective-permute-start | bytes 110600 | tf_op jit(solution)/shard_map/ppermute | solution.py:12
  392.8 1.5 collective-permute-start.7
  394.2 4.7 %collective-permute-done.7 = f32[4,18,1,128]{3,2,1,0:T(1,128)S(1)} collective-permute-done((f32[4,18,1,128]{3,2,1,0:T(1,128)S(1)}, f32[4,18,1,128]{3,2,1,0:T(1,128)S(1)}, u32[]{:S(2)}, u32[]{:S(2)}) %collective-permute-start.7) | collective-permute-done | bytes 36896 | tf_op jit(solution)/shard_map/ppermute | solution.py:15
  400.7 3.2 fusion.4
  (168 shorter events, 139.6 us)
Async XLA Ops:
  6.5 20.5 %copy-start = (bf16[5,5,256,128]{3,2,1,0:T(8,128)(2,1)S(1)}, bf16[5,5,256,128]{3,2,1,0:T(8,128)(2,1)}, u32[]{:S(2)}) copy-start(bf16[5,5,256,128]{3,2,1,0:T(8,128)(2,1)} %param.9) | copy-start | bytes 4915204
  6.5 8.1 %copy-start.1 = (bf16[4,16,16,256]{3,2,1,0:T(8,128)(2,1)S(1)}, bf16[4,16,16,256]{3,2,1,0:T(8,128)(2,1)}, u32[]{:S(2)}) copy-start(bf16[4,16,16,256]{3,2,1,0:T(8,128)(2,1)} %param.8) | copy-start | bytes 1572868
  6.5 132.2 %all-gather.3.cloned.1.call-start = ((), (), s32[]{:S(2)}) async-start(), calls=%async_computation | async-start | bytes 16908288 | tf_op jit(solution)/shard_map/all_gather | solution.py:22
  7.6 7.0 %collective-permute-start = (bf16[4,2,16,256]{3,0,2,1:T(4,128)(2,1)S(1)}, bf16[4,2,16,256]{3,0,2,1:T(4,128)(2,1)S(1)}, u32[]{:S(2)}, u32[]{:S(2)}) collective-permute-start(bf16[4,2,16,256]{3,0,2,1:T(4,128)(2,1)S(1)} %copy.53), channel_id=1, source_target_pairs={{0,2},{1,3},{4,6},{5,7},{8,10},{9,11},{12,14},{13,15},{16,18},{17,... | collective-permute-start | bytes 196616 | tf_op jit(solution)/shard_map/ppermute | solution.py:12
  10.8 5.0 %collective-permute-start.1 = (bf16[4,2,16,256]{3,0,2,1:T(4,128)(2,1)S(1)}, bf16[4,2,16,256]{3,0,2,1:T(4,128)(2,1)S(1)}, u32[]{:S(2)}, u32[]{:S(2)}) collective-permute-start(bf16[4,2,16,256]{3,0,2,1:T(4,128)(2,1)S(1)} %copy.54), channel_id=1, source_target_pairs={{2,0},{3,1},{6,4},{7,5},{10,8},{11,9},{14,12},{15,13},{18,16},{19,... | collective-permute-start | bytes 196616 | tf_op jit(solution)/shard_map/ppermute | solution.py:15
  15.9 5.8 %collective-permute-start.2 = (bf16[4,20,2,256]{3,0,2,1:T(4,128)(2,1)S(1)}, bf16[4,20,2,256]{3,0,2,1:T(4,128)(2,1)S(1)}, u32[]{:S(2)}, u32[]{:S(2)}) collective-permute-start(bf16[4,20,2,256]{3,0,2,1:T(4,128)(2,1)S(1)} %get-tuple-element.130), channel_id=1, source_target_pairs={{0,1},{2,3},{4,5},{6,7},{8,9},{10,11},{12,13},{14,15},{16,17},{18,... | collective-permute-start | bytes 245768 | tf_op jit(solution)/shard_map/ppermute | solution.py:12
  20.3 6.7 %collective-permute-start.3 = (bf16[4,20,2,256]{3,0,2,1:T(4,128)(2,1)S(1)}, bf16[4,20,2,256]{3,0,2,1:T(4,128)(2,1)S(1)}, u32[]{:S(2)}, u32[]{:S(2)}) collective-permute-start(bf16[4,20,2,256]{3,0,2,1:T(4,128)(2,1)S(1)} %get-tuple-element.131), channel_id=1, source_target_pairs={{1,0},{3,2},{5,4},{7,6},{9,8},{11,10},{13,12},{15,14},{17,16},{19,... | collective-permute-start | bytes 245768 | tf_op jit(solution)/shard_map/ppermute | solution.py:15
  21.6 10.8 %copy-start.2 = (f32[128]{0:T(128)S(1)}, f32[128]{0:T(128)}, u32[]{:S(2)}) copy-start(f32[128]{0:T(128)} %param.11) | copy-start | bytes 1540
  33.6 206.5 %all-gather.5.cloned.1.call-start = ((), (), s32[]{:S(2)}) async-start(), calls=%async_computation.1 | async-start | bytes 16908288 | tf_op jit(solution)/shard_map/all_gather | solution.py:22
  380.6 4.4 %collective-permute-start.4 = (f32[4,1,16,128]{3,2,1,0:T(8,128)S(1)}, f32[4,1,16,128]{3,2,1,0:T(8,128)S(1)}, u32[]{:S(2)}, u32[]{:S(2)}) collective-permute-start(f32[4,1,16,128]{3,2,1,0:T(8,128)S(1)} %get-tuple-element.134), channel_id=1, source_target_pairs={{0,2},{1,3},{4,6},{5,7},{8,10},{9,11},{12,14},{13,15},{16,18},{17,... | collective-permute-start | bytes 98312 | tf_op jit(solution)/shard_map/ppermute | solution.py:12
  383.7 4.7 %collective-permute-start.5 = (f32[4,1,16,128]{3,2,1,0:T(8,128)S(1)}, f32[4,1,16,128]{3,2,1,0:T(8,128)S(1)}, u32[]{:S(2)}, u32[]{:S(2)}) collective-permute-start(f32[4,1,16,128]{3,2,1,0:T(8,128)S(1)} %get-tuple-element.135), channel_id=1, source_target_pairs={{2,0},{3,1},{6,4},{7,5},{10,8},{11,9},{14,12},{15,13},{18,16},{19,... | collective-permute-start | bytes 98312 | tf_op jit(solution)/shard_map/ppermute | solution.py:15
  388.4 5.8 %collective-permute-start.6 = (f32[4,18,1,128]{3,2,1,0:T(1,128)S(1)}, f32[4,18,1,128]{3,2,1,0:T(1,128)S(1)}, u32[]{:S(2)}, u32[]{:S(2)}) collective-permute-start(f32[4,18,1,128]{3,2,1,0:T(1,128)S(1)} %get-tuple-element.132), channel_id=1, source_target_pairs={{0,1},{2,3},{4,5},{6,7},{8,9},{10,11},{12,13},{14,15},{16,17},{18,... | collective-permute-start | bytes 110600 | tf_op jit(solution)/shard_map/ppermute | solution.py:12
  392.8 6.2 %collective-permute-start.7 = (f32[4,18,1,128]{3,2,1,0:T(1,128)S(1)}, f32[4,18,1,128]{3,2,1,0:T(1,128)S(1)}, u32[]{:S(2)}, u32[]{:S(2)}) collective-permute-start(f32[4,18,1,128]{3,2,1,0:T(1,128)S(1)} %get-tuple-element.133), channel_id=1, source_target_pairs={{1,0},{3,2},{5,4},{7,6},{9,8},{11,10},{13,12},{15,14},{17,16},{19,... | collective-permute-start | bytes 110600 | tf_op jit(solution)/shard_map/ppermute | solution.py:15
  399.6 1.1 copy-start.4
  399.6 1.1 copy-start.5
  403.9 0.9 copy-start.3
Sparse Core Ops, SparseCore 0:
  33.7 104.9 all-gather.2
  141.8 98.1 all-gather.4
where the time goes:
time: 419 us; the launch traced here: 413 us
  waiting for transfers between devices  221 us (53%)
  other arithmetic  140 us (33%)
  starting transfers between devices  20.3 us (5%)
  between operations  13.7 us (3%)
  matrix products  9.95 us (2%)
  local copies, waits for them, and re-layouts  5.82 us (1%)
    all_gather x2, waiting for transfers between devices, prefix(): everything = jax.tree.map(lambda part: lax.all_gather(part, axis), value)  206 us
    select_n x128, other arithmetic, step(): return jax.tree.map(lambda a, b: jnp.where(reached, a, b), new, before)  137 us
    ppermute x4, starting transfers between devices, with_halo(): lax.ppermute(lax.slice_in_dim(block, block.shape[dim] - width, None, axis...  14.9 us
    ppermute x4, waiting for transfers between devices, with_halo(): lax.ppermute(lax.slice_in_dim(block, 0, width, axis=dim), axis, backward)  14 us
  transfers between devices with their start and end apart: 10, of which 7 were waited for; matrix products, arithmetic and copies ran while one was open for 1% of the time, Pallas kernels for 0%

commit v1 on v0

--- a/solution.py
+++ b/solution.py
@@ -1,7 +1,12 @@
 import jax
 import jax.numpy as jnp
 from jax import lax
+from jax.experimental import pallas as pl
+from jax.experimental.pallas import tpu as pltpu
 from jax.sharding import PartitionSpec as P
+
+ROW = 16
+MESH = pl.DeviceIdType.MESH
 
 
 def with_halo(block, sides, width):
@@ -17,21 +22,106 @@
     return block
 
 
-def prefix(value, axis, combine, identity):
-    length, index = (lax.axis_size(axis), lax.axis_index(axis))
-    everything = jax.tree.map(lambda part: lax.all_gather(part, axis), value)
-    start = jax.tree.map(
-        lambda part, zero: jnp.broadcast_to(jnp.asarray(zero, part.dtype), part.shape),
-        value,
-        identity,
-    )
+def scan_kernel(cols, a_ref, b_ref, o_ref, ra, rb, ca, cb, ta, tb, outs, sems_a, sems_b, sems_ca, sems_cb, sems_o):
+    me = lax.axis_index("tm")
+    r = lax.rem(me, ROW)
+    y = lax.div(me, ROW)
+    base = me - r
+    barrier = pltpu.get_barrier_semaphore()
+    order = [8, 7, 9, 6, 10, 5, 11, 4, 12, 3, 13, 2, 14, 1, 15]
+    peers = [lax.rem(r + d, ROW) for d in order]
+    columns = [lax.rem(y + d, cols) for d in range(1, cols)]
+    for p in peers:
+        pl.semaphore_signal(barrier, inc=1, device_id={"tm": base + p}, device_id_type=MESH)
+    for c in columns:
+        pl.semaphore_signal(barrier, inc=1, device_id={"tm": c * ROW + r}, device_id_type=MESH)
+    pl.semaphore_wait(barrier, ROW - 1 + cols - 1)
 
-    def step(k, before):
-        reached = k < index
-        new = combine(before, jax.tree.map(lambda part: part[k], everything))
-        return jax.tree.map(lambda a, b: jnp.where(reached, a, b), new, before)
+    def row_copy(src, dst, sems, p):
+        return pltpu.make_async_remote_copy(
+            src_ref=src, dst_ref=dst, send_sem=sems.at[0, p], recv_sem=sems.at[1, r],
+            device_id={"tm": base + p}, device_id_type=MESH)
 
-    return lax.fori_loop(0, length, step, start)
+    def row_arrival(src, dst, sems, p):
+        return pltpu.make_async_remote_copy(
+            src_ref=src, dst_ref=dst, send_sem=sems.at[0, p], recv_sem=sems.at[1, p],
+            device_id={"tm": base + p}, device_id_type=MESH)
+
+    for p in peers:
+        row_copy(a_ref.at[p], ra.at[r], sems_a, p).start()
+        row_copy(b_ref.at[p], rb.at[r], sems_b, p).start()
+    ra[r] = a_ref[r]
+    rb[r] = b_ref[r]
+    for p in peers:
+        row_arrival(a_ref.at[p], ra.at[p], sems_a, p).wait()
+        row_arrival(b_ref.at[p], rb.at[p], sems_b, p).wait()
+    total_a = jnp.ones_like(ra[0])
+    total_b = jnp.zeros_like(rb[0])
+    before = []
+    for k in range(ROW):
+        before.append((total_a, total_b))
+        here = ra[k]
+        total_b = here * total_b + rb[k]
+        total_a = total_a * here
+    ta[...] = total_a
+    tb[...] = total_b
+
+    def column_copy(src, dst, sems, c, slot):
+        return pltpu.make_async_remote_copy(
+            src_ref=src, dst_ref=dst, send_sem=sems.at[0, c], recv_sem=sems.at[1, slot],
+            device_id={"tm": c * ROW + r}, device_id_type=MESH)
+
+    for c in columns:
+        column_copy(ta, ca.at[y], sems_ca, c, y).start()
+        column_copy(tb, cb.at[y], sems_cb, c, y).start()
+    ca[y] = total_a
+    cb[y] = total_b
+    for c in columns:
+        column_copy(ta, ca.at[c], sems_ca, c, c).wait()
+        column_copy(tb, cb.at[c], sems_cb, c, c).wait()
+    carry = jnp.zeros_like(total_b)
+    for c in range(cols):
+        carry = jnp.where(c < y, ca[c] * carry + cb[c], carry)
+    for k in range(ROW):
+        outs[k] = before[k][0] * carry + before[k][1]
+    for p in peers:
+        row_copy(outs.at[p], o_ref.at[r], sems_o, p).start()
+    o_ref[r] = outs[r]
+    for p in peers:
+        row_arrival(outs.at[p], o_ref.at[p], sems_o, p).wait()
+
+
+def prefix(decay, state):
+    cols = lax.axis_size("tm") // ROW
+    shape = (ROW, state.shape[0] * state.shape[1] // ROW, state.shape[2])
+    chunk = shape[1:]
+    vmem = pl.BlockSpec(memory_space=pltpu.VMEM)
+
+    def kernel(*refs):
+        scan_kernel(cols, *refs)
+
+    result = pl.pallas_call(
+        kernel,
+        out_shape=jax.ShapeDtypeStruct(shape, jnp.float32),
+        in_specs=[vmem, vmem],
+        out_specs=vmem,
+        scratch_shapes=[
+            pltpu.VMEM((ROW,) + chunk, jnp.float32),
+            pltpu.VMEM((ROW,) + chunk, jnp.float32),
+            pltpu.VMEM((cols,) + chunk, jnp.float32),
+            pltpu.VMEM((cols,) + chunk, jnp.float32),
+            pltpu.VMEM(chunk, jnp.float32),
+            pltpu.VMEM(chunk, jnp.float32),
+            pltpu.VMEM((ROW,) + chunk, jnp.float32),
+            pltpu.SemaphoreType.DMA((2, ROW)),
+            pltpu.SemaphoreType.DMA((2, ROW)),
+            pltpu.SemaphoreType.DMA((2, cols)),
+            pltpu.SemaphoreType.DMA((2, cols)),
+            pltpu.SemaphoreType.DMA((2, ROW)),
+        ],
+        compiler_params=pltpu.CompilerParams(collective_id=0, has_side_effects=True),
+    )(decay.reshape(shape), state.reshape(shape))
+    return result.reshape(state.shape)
 
 
 def convolve(padded, kernel):
@@ -72,13 +162,8 @@
         summed = summed + step[frame]
         locals_list.append(state)
         summed_list.append(summed)
-
-    def compose(earlier, later):
-        return (earlier[0] * later[0], later[0] * earlier[1] + later[1])
-
     product = jnp.exp(-summed[..., None] * rates)
-    identity = (jnp.ones_like(product), jnp.zeros_like(state))
-    _, incoming = prefix((product, state), "tm", compose, identity)
+    incoming = prefix(product, state)
     hidden_list = []
     for frame in range(count):
         fixed = locals_list[frame] + jnp.exp(-summed_list[frame][..., None] * rates) * incoming

time: 419 us -> 90.8 us (0.22)
  the two profiles are of different devices: /device:TPU:57 before, /device:TPU:64 now
where the time goes in v1:
time: 90.8 us; the launch traced here: 90.4 us
  Pallas kernels  34.5 us (38%)
  waiting for transfers between devices  18.8 us (21%)
  starting transfers between devices  17.8 us (20%)
  matrix products  9.93 us (11%)
  local copies, waits for them, and re-layouts  5.82 us (6%)
  other arithmetic  3.37 us (4%)
    pallas_call x1, Pallas kernels, prefix(): pl.pallas_call(kernel, out_shape=jax.ShapeDtypeStruct(shape, jnp.float32)...  34.5 us
    ppermute x4, waiting for transfers between devices, with_halo(): lax.ppermute(lax.slice_in_dim(block, 0, width, axis=dim), axis, backward)  17.7 us
    ppermute x4, starting transfers between devices, with_halo(): lax.ppermute(lax.slice_in_dim(block, block.shape[dim] - width, None, axis...  12.4 us
    ppermute x4, starting transfers between devices, with_halo(): lax.ppermute(lax.slice_in_dim(block, 0, width, axis=dim), axis, backward)  5.35 us
    conv_general_dilated x1, matrix products, convolve(): lax.conv_general_dilated(padded, kernel, (1, 1), 'VALID', dimension_numbe...  4.98 us
    conv_general_dilated x1, matrix products, convolve_exact(): lax.conv_general_dilated(padded, kernel.astype(jnp.float32), (1, 1), 'VAL...  3.21 us
    unnamed x18, local copies, waits for them, and re-layouts  2.2 us
  transfers between devices with their start and end apart: 8, of which 7 were waited for; matrix products, arithmetic and copies ran while one was open for 3% of the time, Pallas kernels for 0%

profile of v1, /device:TPU:64, one launch (start us, length us, event | category | flops | bytes accessed | tf_op | source)
XLA Modules:
  0.0 90.4 jit_solution(1038949203421122139)
XLA Ops:
  0.0 1.0 %fusion.51 = (bf16[4,2,16,256]{3,2,1,0:T(8,128)(2,1)S(1)}, bf16[4,2,16,256]{3,2,1,0:T(8,128)(2,1)S(1)}) fusion(bf16[4,16,16,256]{3,2,1,0:T(8,128)(2,1)} %param.6), kind=kLoop, calls=%fused_computation.85 | loop fusion | bytes 262144 | tf_op jit(solution)/shard_map/slice | solution.py:20
  1.1 3.4 %collective-permute-start = (bf16[4,2,16,256]{3,0,2,1:T(4,128)(2,1)S(1)}, bf16[4,2,16,256]{3,0,2,1:T(4,128)(2,1)S(1)}, u32[]{:S(2)}, u32[]{:S(2)}) collective-permute-start(bf16[4,2,16,256]{3,0,2,1:T(4,128)(2,1)S(1)} %copy.42), channel_id=1, source_target_pairs={{0,2},{1,3},{4,6},{5,7},{8,10},{9,11},{12,14},{13,15},{16,18},{17,... | collective-permute-start | bytes 196616 | tf_op jit(solution)/shard_map/ppermute | solution.py:17
  4.6 1.3 %collective-permute-start.1 = (bf16[4,2,16,256]{3,0,2,1:T(4,128)(2,1)S(1)}, bf16[4,2,16,256]{3,0,2,1:T(4,128)(2,1)S(1)}, u32[]{:S(2)}, u32[]{:S(2)}) collective-permute-start(bf16[4,2,16,256]{3,0,2,1:T(4,128)(2,1)S(1)} %copy.43), channel_id=1, source_target_pairs={{2,0},{3,1},{6,4},{7,5},{10,8},{11,9},{14,12},{15,13},{18,16},{19,... | collective-permute-start | bytes 196616 | tf_op jit(solution)/shard_map/ppermute | solution.py:20
  5.9 0.7 reshape.63
  6.5 1.7 %fusion.42 = f32[1,4,16,16]{3,0,2,1:T(1,128)S(1)} fusion(bf16[4,16,16,256]{3,2,1,0:T(8,128)(2,1)} %param.6, bf16[256,1,1,1]{0,1,2,3:T(2,128)(2,1)S(1)} %reshape.63), kind=kOutput, calls=%fused_computation.77 | convolution fusion | flops 524288 | bytes 528896 | tf_op jit(solution)/shard_map/dot_general | solution.py:153
  8.8 1.9 %collective-permute-done.1 = bf16[4,2,16,256]{3,0,2,1:T(4,128)(2,1)S(1)} collective-permute-done((bf16[4,2,16,256]{3,0,2,1:T(4,128)(2,1)S(1)}, bf16[4,2,16,256]{3,0,2,1:T(4,128)(2,1)S(1)}, u32[]{:S(2)}, u32[]{:S(2)}) %collective-permute-start.1) | collective-permute-done | bytes 65568 | tf_op jit(solution)/shard_map/ppermute | solution.py:20
  10.8 4.6 %collective-permute-start.2 = (bf16[4,20,2,256]{3,0,2,1:T(4,128)(2,1)S(1)}, bf16[4,20,2,256]{3,0,2,1:T(4,128)(2,1)S(1)}, u32[]{:S(2)}, u32[]{:S(2)}) collective-permute-start(bf16[4,20,2,256]{3,0,2,1:T(4,128)(2,1)S(1)} %get-tuple-element.7), channel_id=1, source_target_pairs={{0,1},{2,3},{4,5},{6,7},{8,9},{10,11},{12,13},{14,15},{16,17},{18,... | collective-permute-start | bytes 245768 | tf_op jit(solution)/shard_map/ppermute | solution.py:17
  15.5 1.3 %collective-permute-start.3 = (bf16[4,20,2,256]{3,0,2,1:T(4,128)(2,1)S(1)}, bf16[4,20,2,256]{3,0,2,1:T(4,128)(2,1)S(1)}, u32[]{:S(2)}, u32[]{:S(2)}) collective-permute-start(bf16[4,20,2,256]{3,0,2,1:T(4,128)(2,1)S(1)} %get-tuple-element.8), channel_id=1, source_target_pairs={{1,0},{3,2},{5,4},{7,6},{9,8},{11,10},{13,12},{15,14},{17,16},{19,... | collective-permute-start | bytes 245768 | tf_op jit(solution)/shard_map/ppermute | solution.py:20
  16.8 0.7 collective-permute-done.2
  17.5 5.8 %collective-permute-done.3 = bf16[4,20,2,256]{3,0,2,1:T(4,128)(2,1)S(1)} collective-permute-done((bf16[4,20,2,256]{3,0,2,1:T(4,128)(2,1)S(1)}, bf16[4,20,2,256]{3,0,2,1:T(4,128)(2,1)S(1)}, u32[]{:S(2)}, u32[]{:S(2)}) %collective-permute-start.3) | collective-permute-done | bytes 81952 | tf_op jit(solution)/shard_map/ppermute | solution.py:20
  23.3 5.0 %fusion.8 = f32[4,16,16,128]{3,0,2,1:T(4,128)S(1)} fusion(bf16[5,5,256,128]{3,2,1,0:T(8,128)(2,1)S(1)} %copy-done, bf16[4,20,2,256]{3,0,2,1:T(4,128)(2,1)S(1)} %collective-permute-done.3, bf16[4,20,16,256]{3,0,2,1:T(4,128)(2,1)S(1)} %constant_dynamic-update-slice_fusion, bf16[4,20,2,256]{3,0,2,1:T(4,128)(2,1)S(1)} %collective-permute-done.2), kind=kOutput, calls=%fused_computation.10 | convolution fusion | flops 1680179200 | bytes 2981888 | tf_op jit(solution)/shard_map/conv_general_dilated | solution.py:128
  28.7 1.2 %fusion.23 = (f32[16,16,128]{2,1,0:T(8,128)}, f32[16,16,128]{2,1,0:T(8,128)S(1)}, f32[16,16,128]{2,1,0:T(8,128)}) fusion(f32[16,16,128]{2,1,0:T(8,128)S(1)} %bitcast.83, f32[16,16]{1,0:T(8,128)S(1)} %get-tuple-element.30, f32[128]{0:T(128)S(1)} %copy-done.2, f32[16,16,128]{2,1,0:T(8,128)S(1)} %bitcast.80, f32[16,16]{1,0:T(8,128)S(1)} %get-tuple-element.31, ...), kind=kLoop, calls=%fused_computation.33 | loop fusion | flops 950272 | bytes 923136 | tf_op jit(solution)/shard_map/add | solution.py:161
  29.9 34.5 %shard_map.64 = f32[16,16,128]{2,1,0:T(8,128)} custom-call(f32[16,16,128]{2,1,0:T(8,128)} %get-tuple-element.33.refs_0_, f32[16,16,128]{2,1,0:T(8,128)} %get-tuple-element.5.refs_1_), custom_call_target="tpu_custom_call" | custom-call | tf_op jit(solution)/shard_map/pallas_call | solution.py:103
  64.4 1.3 %add_bitcast_fusion.3 = (f32[1,16,16,128]{3,2,1,0:T(8,128)S(1)}, f32[1,16,16,128]{3,2,1,0:T(8,128)S(1)}, f32[1,16,16,128]{3,2,1,0:T(8,128)S(1)}, f32[1,16,16,128]{3,2,1,0:T(8,128)S(1)}) fusion(f32[16,16,128]{2,1,0:T(8,128)} %shard_map.64, f32[16,16]{1,0:T(8,128)S(1)} %get-tuple-element.25, f32[128]{0:T(128)S(1)} %copy-done.2, ...), kind=kLoop, calls=%fused_computation.55 | loop fusion | flops 851968 | bytes 1186304 | tf_op jit(solution)/shard_map/stack | solution.py:171
  65.7 2.1 %collective-permute-start.4 = (f32[4,1,16,128]{3,2,1,0:T(8,128)S(1)}, f32[4,1,16,128]{3,2,1,0:T(8,128)S(1)}, u32[]{:S(2)}, u32[]{:S(2)}) collective-permute-start(f32[4,1,16,128]{3,2,1,0:T(8,128)S(1)} %get-tuple-element.11), channel_id=1, source_target_pairs={{0,2},{1,3},{4,6},{5,7},{8,10},{9,11},{12,14},{13,15},{16,18},{17,... | collective-permute-start | bytes 98312 | tf_op jit(solution)/shard_map/ppermute | solution.py:17
  67.8 1.3 %collective-permute-start.5 = (f32[4,1,16,128]{3,2,1,0:T(8,128)S(1)}, f32[4,1,16,128]{3,2,1,0:T(8,128)S(1)}, u32[]{:S(2)}, u32[]{:S(2)}) collective-permute-start(f32[4,1,16,128]{3,2,1,0:T(8,128)S(1)} %get-tuple-element.12), channel_id=1, source_target_pairs={{2,0},{3,1},{6,4},{7,5},{10,8},{11,9},{14,12},{15,13},{18,16},{19,... | collective-permute-start | bytes 98312 | tf_op jit(solution)/shard_map/ppermute | solution.py:20
  69.3 4.2 %collective-permute-done.5 = f32[4,1,16,128]{3,2,1,0:T(8,128)S(1)} collective-permute-done((f32[4,1,16,128]{3,2,1,0:T(8,128)S(1)}, f32[4,1,16,128]{3,2,1,0:T(8,128)S(1)}, u32[]{:S(2)}, u32[]{:S(2)}) %collective-permute-start.5) | collective-permute-done | bytes 32800 | tf_op jit(solution)/shard_map/ppermute | solution.py:20
  73.6 2.3 %collective-permute-start.6 = (f32[4,18,1,128]{3,2,1,0:T(1,128)S(1)}, f32[4,18,1,128]{3,2,1,0:T(1,128)S(1)}, u32[]{:S(2)}, u32[]{:S(2)}) collective-permute-start(f32[4,18,1,128]{3,2,1,0:T(1,128)S(1)} %get-tuple-element.9), channel_id=1, source_target_pairs={{0,1},{2,3},{4,5},{6,7},{8,9},{10,11},{12,13},{14,15},{16,17},{18,... | collective-permute-start | bytes 110600 | tf_op jit(solution)/shard_map/ppermute | solution.py:17
  76.0 1.5 %collective-permute-start.7 = (f32[4,18,1,128]{3,2,1,0:T(1,128)S(1)}, f32[4,18,1,128]{3,2,1,0:T(1,128)S(1)}, u32[]{:S(2)}, u32[]{:S(2)}) collective-permute-start(f32[4,18,1,128]{3,2,1,0:T(1,128)S(1)} %get-tuple-element.10), channel_id=1, source_target_pairs={{1,0},{3,2},{5,4},{7,6},{9,8},{11,10},{13,12},{15,14},{17,16},{19,... | collective-permute-start | bytes 110600 | tf_op jit(solution)/shard_map/ppermute | solution.py:20
  77.6 5.7 %collective-permute-done.7 = f32[4,18,1,128]{3,2,1,0:T(1,128)S(1)} collective-permute-done((f32[4,18,1,128]{3,2,1,0:T(1,128)S(1)}, f32[4,18,1,128]{3,2,1,0:T(1,128)S(1)}, u32[]{:S(2)}, u32[]{:S(2)}) %collective-permute-start.7) | collective-permute-done | bytes 36896 | tf_op jit(solution)/shard_map/ppermute | solution.py:20
  84.4 0.7 copy-done.4
  85.0 3.2 %fusion.3 = f32[16,32,3,256]{3,1,2,0:T(8,128)S(1)} fusion(bf16[3,3,128,256]{3,2,1,0:T(8,128)(2,1)S(1)} %copy-done.4, f32[18,4,8,5,128]{4,1,3,2,0:T(4,128)S(1)} %select_maximum_fusion, pred[32,3]{0,1:T(4,128)(4,1)S(1)} %copy-done.5), kind=kOutput, calls=%fused_computation.5 | convolution fusion | flops 5436211200 | bytes 3637344 | tf_op jit(solution)/shard_map/conv_general_dilated | solution.py:139
  88.3 0.9 %copy.24 = f32[16,32,3,256]{3,0,2,1:T(8,128)S(1)} copy(f32[16,32,3,256]{3,1,2,0:T(8,128)S(1)} %fusion.3) | data formatting | bytes 3145728 | tf_op jit(solution)/shard_map/conv_general_dilated | solution.py:139
  89.5 1.0 %copy.26 = bf16[4,16,16,256]{3,2,1,0:T(8,128)(2,1)} copy(bf16[4,16,16,256]{3,1,2,0:T(8,128)(2,1)S(1)} %fusion.7) | data formatting | bytes 1048576 | tf_op jit(solution)/shard_map/convert_element_type | solution.py:174
  (32 shorter events, 2.9 us)
Async XLA Ops:
  0.0 23.3 %copy-start = (bf16[5,5,256,128]{3,2,1,0:T(8,128)(2,1)S(1)}, bf16[5,5,256,128]{3,2,1,0:T(8,128)(2,1)}, u32[]{:S(2)}) copy-start(bf16[5,5,256,128]{3,2,1,0:T(8,128)(2,1)} %param.7) | copy-start | bytes 4915204
  0.0 8.4 %copy-start.1 = (bf16[4,16,16,256]{3,2,1,0:T(8,128)(2,1)S(1)}, bf16[4,16,16,256]{3,2,1,0:T(8,128)(2,1)}, u32[]{:S(2)}) copy-start(bf16[4,16,16,256]{3,2,1,0:T(8,128)(2,1)} %param.6) | copy-start | bytes 1572868
  1.1 7.2 %collective-permute-start = (bf16[4,2,16,256]{3,0,2,1:T(4,128)(2,1)S(1)}, bf16[4,2,16,256]{3,0,2,1:T(4,128)(2,1)S(1)}, u32[]{:S(2)}, u32[]{:S(2)}) collective-permute-start(bf16[4,2,16,256]{3,0,2,1:T(4,128)(2,1)S(1)} %copy.42), channel_id=1, source_target_pairs={{0,2},{1,3},{4,6},{5,7},{8,10},{9,11},{12,14},{13,15},{16,18},{17,... | collective-permute-start | bytes 196616 | tf_op jit(solution)/shard_map/ppermute | solution.py:17
  4.6 6.2 %collective-permute-start.1 = (bf16[4,2,16,256]{3,0,2,1:T(4,128)(2,1)S(1)}, bf16[4,2,16,256]{3,0,2,1:T(4,128)(2,1)S(1)}, u32[]{:S(2)}, u32[]{:S(2)}) collective-permute-start(bf16[4,2,16,256]{3,0,2,1:T(4,128)(2,1)S(1)} %copy.43), channel_id=1, source_target_pairs={{2,0},{3,1},{6,4},{7,5},{10,8},{11,9},{14,12},{15,13},{18,16},{19,... | collective-permute-start | bytes 196616 | tf_op jit(solution)/shard_map/ppermute | solution.py:20
  10.8 6.7 %collective-permute-start.2 = (bf16[4,20,2,256]{3,0,2,1:T(4,128)(2,1)S(1)}, bf16[4,20,2,256]{3,0,2,1:T(4,128)(2,1)S(1)}, u32[]{:S(2)}, u32[]{:S(2)}) collective-permute-start(bf16[4,20,2,256]{3,0,2,1:T(4,128)(2,1)S(1)} %get-tuple-element.7), channel_id=1, source_target_pairs={{0,1},{2,3},{4,5},{6,7},{8,9},{10,11},{12,13},{14,15},{16,17},{18,... | collective-permute-start | bytes 245768 | tf_op jit(solution)/shard_map/ppermute | solution.py:17
  15.5 7.8 %collective-permute-start.3 = (bf16[4,20,2,256]{3,0,2,1:T(4,128)(2,1)S(1)}, bf16[4,20,2,256]{3,0,2,1:T(4,128)(2,1)S(1)}, u32[]{:S(2)}, u32[]{:S(2)}) collective-permute-start(bf16[4,20,2,256]{3,0,2,1:T(4,128)(2,1)S(1)} %get-tuple-element.8), channel_id=1, source_target_pairs={{1,0},{3,2},{5,4},{7,6},{9,8},{11,10},{13,12},{15,14},{17,16},{19,... | collective-permute-start | bytes 245768 | tf_op jit(solution)/shard_map/ppermute | solution.py:20
  16.8 11.9 %copy-start.2 = (f32[128]{0:T(128)S(1)}, f32[128]{0:T(128)}, u32[]{:S(2)}) copy-start(f32[128]{0:T(128)} %param.9) | copy-start | bytes 1540
  65.7 3.6 %collective-permute-start.4 = (f32[4,1,16,128]{3,2,1,0:T(8,128)S(1)}, f32[4,1,16,128]{3,2,1,0:T(8,128)S(1)}, u32[]{:S(2)}, u32[]{:S(2)}) collective-permute-start(f32[4,1,16,128]{3,2,1,0:T(8,128)S(1)} %get-tuple-element.11), channel_id=1, source_target_pairs={{0,2},{1,3},{4,6},{5,7},{8,10},{9,11},{12,14},{13,15},{16,18},{17,... | collective-permute-start | bytes 98312 | tf_op jit(solution)/shard_map/ppermute | solution.py:17
  67.8 5.8 %collective-permute-start.5 = (f32[4,1,16,128]{3,2,1,0:T(8,128)S(1)}, f32[4,1,16,128]{3,2,1,0:T(8,128)S(1)}, u32[]{:S(2)}, u32[]{:S(2)}) collective-permute-start(f32[4,1,16,128]{3,2,1,0:T(8,128)S(1)} %get-tuple-element.12), channel_id=1, source_target_pairs={{2,0},{3,1},{6,4},{7,5},{10,8},{11,9},{14,12},{15,13},{18,16},{19,... | collective-permute-start | bytes 98312 | tf_op jit(solution)/shard_map/ppermute | solution.py:20
  73.6 3.9 %collective-permute-start.6 = (f32[4,18,1,128]{3,2,1,0:T(1,128)S(1)}, f32[4,18,1,128]{3,2,1,0:T(1,128)S(1)}, u32[]{:S(2)}, u32[]{:S(2)}) collective-permute-start(f32[4,18,1,128]{3,2,1,0:T(1,128)S(1)} %get-tuple-element.9), channel_id=1, source_target_pairs={{0,1},{2,3},{4,5},{6,7},{8,9},{10,11},{12,13},{14,15},{16,17},{18,... | collective-permute-start | bytes 110600 | tf_op jit(solution)/shard_map/ppermute | solution.py:17
  76.0 7.4 %collective-permute-start.7 = (f32[4,18,1,128]{3,2,1,0:T(1,128)S(1)}, f32[4,18,1,128]{3,2,1,0:T(1,128)S(1)}, u32[]{:S(2)}, u32[]{:S(2)}) collective-permute-start(f32[4,18,1,128]{3,2,1,0:T(1,128)S(1)} %get-tuple-element.10), channel_id=1, source_target_pairs={{1,0},{3,2},{5,4},{7,6},{9,8},{11,10},{13,12},{15,14},{17,16},{19,... | collective-permute-start | bytes 110600 | tf_op jit(solution)/shard_map/ppermute | solution.py:20
  84.0 1.1 %copy-start.4 = (bf16[3,3,128,256]{3,2,1,0:T(8,128)(2,1)S(1)}, bf16[3,3,128,256]{3,2,1,0:T(8,128)(2,1)}, u32[]{:S(2)}) copy-start(bf16[3,3,128,256]{3,2,1,0:T(8,128)(2,1)} %param.10) | copy-start | bytes 1769476
  84.0 1.1 %copy-start.5 = (pred[32,3]{0,1:T(4,128)(4,1)S(1)}, pred[32,3]{0,1:T(4,128)(4,1)}, u32[]{:S(2)}) copy-start(pred[32,3]{0,1:T(4,128)(4,1)} %constant.11) | copy-start | bytes 292
  88.3 0.9 %copy-start.3 = (f32[256]{0:T(256)S(1)}, f32[256]{0:T(256)}, u32[]{:S(2)}) copy-start(f32[256]{0:T(256)} %param.11) | copy-start | bytes 3076

commit v2 on v0

v2 whole, which is shorter than its diff:
```python
import jax
import jax.numpy as jnp
from jax import lax
from jax.experimental import pallas as pl
from jax.experimental.pallas import tpu as pltpu
from jax.sharding import PartitionSpec as P

ROW = 16
T, H, W = 4, 16, 16
PIX = H * W
C, S = 256, 128
MESH = pl.DeviceIdType.MESH
ORDER = [8, 7, 9, 6, 10, 5, 11, 4, 12, 3, 13, 2, 14, 1, 15]
F32 = jnp.float32
BF16 = jnp.bfloat16


def dot(a, b):
    return jnp.dot(a, b, preferred_element_type=F32)


def shifted(wide, taps, width, reach):
    rows = wide.shape[0]
    column = lax.rem(lax.broadcasted_iota(jnp.int32, (rows, width), 0), W)
    total = wide[:, reach * width:(reach + 1) * width]
    for tap in range(taps):
        move = tap - reach
        if move == 0:
            continue
        part = pltpu.roll(wide[:, tap * width:(tap + 1) * width], (-move) % rows, 0)
        inside = (column + move >= 0) & (column + move < W)
        total = total + jnp.where(inside, part, 0.0)
    return total


def one_minus_exp(u):
    series = u * (1.0 - u * (1 / 2) * (1.0 - u * (1 / 3) * (1.0 - u * (1 / 4) * (1.0 - u * (1 / 5) * (
        1.0 - u * (1 / 6) * (1.0 - u * (1 / 7) * (1.0 - u * (1 / 8))))))))
    return jnp.where(u < 0.5, series, 1.0 - jnp.exp(-u))


def layer_kernel(cols, frames, w1, dt, rates, w2, skip, out,
                 xp, wc, wc2, hr, hc, sc, gain, fade, drive, loc, hid, hr2, hc2, sc2, acc,
                 sa, sb, ra, rb, ca, cb, ta, tb, so, inc,
                 load, wload, w2load, halo, halo2, sems_a, sems_b, sems_ca, sems_cb, sems_o):
    me = lax.axis_index("tm")
    sy = lax.axis_index("sy")
    sx = lax.axis_index("sx")
    r = lax.rem(me, ROW)
    y = lax.div(me, ROW)
    base = me - r
    peers = [lax.rem(r + d, ROW) for d in ORDER]
    columns = [lax.rem(y + d, cols) for d in (4, 3, 5, 2, 6, 1, 7) if d < cols]
    near = [{"sy": 1 - sy}, {"sx": 1 - sx}, {"sy": 1 - sy, "sx": 1 - sx}]

    loads = [pltpu.make_async_copy(frames, xp.at[:, pl.ds(2, H)], load)]
    loads[0].start()
    wloads = []
    for i in range(25):
        wloads.append(pltpu.make_async_copy(
            w1.at[i], wc.at[pl.ds((i // 5) * C, C), pl.ds((i % 5) * S, S)], wload.at[i]))
    for c in wloads:
        c.start()
    w2loads = []
    for i in range(9):
        for half in range(2):
            w2loads.append(pltpu.make_async_copy(
                w2.at[i], wc2.at[pl.ds((i // 3) * C + half * S, S), pl.ds((i % 3) * C, C)],
                w2load.at[2 * i + half]))
    for c in w2loads:
        c.start()

    zrow = jnp.zeros((W, C), BF16)
    for f in range(T):
        for row in (0, 1, 18, 19):
            xp[f, row] = zrow
        hr[f, 2 * sy] = zrow
        hid[f, 0] = zrow
        hid[f, 17] = zrow
    for row in range(2):
        hc[18 * sy + row] = zrow
    hc2[17 * sy] = zrow

    barrier = pltpu.get_barrier_semaphore()
    targets = near + [{"tm": base + p} for p in peers] + [{"tm": c * ROW + r} for c in columns]
    for where in targets:
        pl.semaphore_signal(barrier, inc=1, device_id=where, device_id_type=MESH)

    loads[0].wait()
    row_id = lax.broadcasted_iota(jnp.int32, (PIX, 1), 0)
    slot = lax.rem(row_id, 16)
    edge = jnp.where(sx == 0, 15 - slot // 4, slot // 4)
    target = jnp.where(slot < 8, lax.rem(slot, 4) * PIX + (row_id // 16) * W + edge, -1)
    lane = lax.broadcasted_iota(jnp.int32, (PIX, PIX), 1)
    picked = jnp.zeros((PIX, C), F32)
    for f in range(T):
        pick = jnp.where(lane + f * PIX == target, 1.0, 0.0).astype(BF16)
        picked = picked + dot(pick, xp[f, pl.ds(2, H)].reshape(PIX, C))
    sc[...] = picked.astype(BF16).reshape(H, 16, C)

    def send(src, dst, sems, slot_out, slot_in, where):
        return pltpu.make_async_remote_copy(
            src_ref=src, dst_ref=dst, send_sem=sems.at[0, slot_out], recv_sem=sems.at[1, slot_in],
            device_id=where, device_id_type=MESH)

    pl.semaphore_wait(barrier, len(targets))
    halo_copies = [
        send(frames.at[:, pl.ds(14 * (1 - sy), 2)], hr.at[:, pl.ds(sy, 2)], halo, 0, 0, near[0]),
        send(sc, hc.at[pl.ds(2, H)], halo, 1, 1, near[1]),
        send(sc.at[pl.ds(14 * (1 - sy), 2)], hc.at[pl.ds(18 * sy, 2)], halo, 2, 2, near[2]),
    ]
    for c in halo_copies:
        c.start()

    weight = jnp.broadcast_to(dt[...].reshape(1, C), (S, C))
    speed = rates[...]
    faded = None
    for f in range(T):
        v = lax.dot_general(xp[f, pl.ds(2, H)].reshape(PIX, C), weight, (((1,), (1,)), ((), ())),
                            preferred_element_type=F32)
        scaled = (jnp.maximum(v, 0.0) + jnp.log1p(jnp.exp(-jnp.abs(v)))) * speed
        decay = jnp.exp(-scaled)
        gain[f] = jnp.sqrt(one_minus_exp(2.0 * scaled))
        loc[f] = decay
        faded = decay if f == 0 else faded * decay
        fade[f] = faded
    sa[...] = faded.reshape(ROW, H, S)
    for p in peers:
        send(sa.at[p], ra.at[r], sems_a, p, r, {"tm": base + p}).start()
    ra[r] = sa[r]

    for c in wloads:
        c.wait()
    for f in range(T):
        left = jnp.concatenate([xp[f, pl.ds(dy, H)].reshape(PIX, C) for dy in range(5)], axis=1)
        drive[f] = shifted(dot(left, wc[...]), 5, S, 2)

    for c in halo_copies:
        c.wait()
    left = jnp.concatenate([hr[:, pl.ds(k, 2)].reshape(T * 2 * W, C) for k in range(2)], axis=1)
    first = pl.multiple_of(3 * C * (1 - sy), C)
    extra = shifted(dot(left, wc[pl.ds(first, 2 * C), :]), 5, S, 2).reshape(T, 2 * W, S)
    at = pl.multiple_of(14 * W * (1 - sy), 2 * W)
    for f in range(T):
        drive[f, pl.ds(at, 2 * W), :] += extra[f]
    left = jnp.concatenate([hc[pl.ds(dy, H)].reshape(PIX, C) for dy in range(5)], axis=1)
    first = pl.multiple_of(3 * S * (1 - sx), S)
    side = dot(left, wc[:, pl.ds(first, 2 * S)]).reshape(H, 16, 2 * S)
    close = jnp.where(sx == 0, side[:, :, :S], side[:, :, S:])
    far = jnp.where(sx == 0, side[:, :, S:], side[:, :, :S])
    lane8 = lax.broadcasted_iota(jnp.int32, (1, 8, S), 1)
    outer = lane8 == 7 * (1 - sx)
    inner = lane8 == 5 * (1 - sx) + 1
    at = pl.multiple_of(8 * (1 - sx), 8)
    drive4 = drive.reshape(T, H, W, S)
    for f in range(T):
        add = jnp.where(outer, close[:, f:f + 1, :] + far[:, 4 + f:5 + f, :], 0.0)
        add = add + jnp.where(inner, far[:, f:f + 1, :], 0.0)
        drive4[f, :, pl.ds(at, 8), :] += add

    state = gain[0] * drive[0]
    for f in range(1, T):
        decay = loc[f]
        loc[f - 1] = state
        state = decay * state + gain[f] * drive[f]
    loc[T - 1] = state
    sb[...] = state.reshape(ROW, H, S)
    for p in peers:
        send(sb.at[p], rb.at[r], sems_b, p, r, {"tm": base + p}).start()
    rb[r] = sb[r]

    for p in peers:
        send(sa.at[p], ra.at[p], sems_a, p, p, {"tm": base + p}).wait()
    total_a = ra[0]
    for k in range(1, ROW):
        total_a = total_a * ra[k]
    ta[...] = total_a
    for c in columns:
        send(ta, ca.at[y], sems_ca, c, y, {"tm": c * ROW + r}).start()
    for c in w2loads:
        c.wait()

    for p in peers:
        send(sb.at[p], rb.at[p], sems_b, p, p, {"tm": base + p}).wait()
    total_b = rb[0]
    for k in range(1, ROW):
        total_b = ra[k] * total_b + rb[k]
    tb[...] = total_b
    for c in columns:
        send(tb, cb.at[y], sems_cb, c, y, {"tm": c * ROW + r}).start()
    for c in columns:
        send(ta, ca.at[c], sems_ca, c, c, {"tm": c * ROW + r}).wait()
    for c in columns:
        send(tb, cb.at[c], sems_cb, c, c, {"tm": c * ROW + r}).wait()
    ca[y] = total_a
    cb[y] = total_b
    carry = jnp.zeros_like(total_b)
    for c in range(cols):
        carry = jnp.where(c < y, ca[c] * carry + cb[c], carry)
    so[0] = carry
    for k in range(ROW - 1):
        carry = ra[k] * carry + rb[k]
        so[k + 1] = carry
    for p in peers:
        send(so.at[p], inc.at[r], sems_o, p, r, {"tm": base + p}).start()
    inc[r] = so[r]
    for p in peers:
        send(so.at[p], inc.at[p], sems_o, p, p, {"tm": base + p}).wait()

    before = inc[...].reshape(PIX, S)
    for f in range(T):
        state = loc[f] + fade[f] * before
        high = state.astype(BF16)
        low = (state - high.astype(F32)).astype(BF16)
        hid[f, pl.ds(1, H)] = jnp.concatenate([high, low], axis=1).reshape(H, W, C)
    edge = 15 * (1 - sx)
    target = jnp.where(slot < 4, slot * PIX + (row_id // 16) * W + edge, -1)
    picked = jnp.zeros((PIX, C), F32)
    for f in range(T):
        pick = jnp.where(lane + f * PIX == target, 1.0, 0.0).astype(BF16)
        picked = picked + dot(pick, hid[f, pl.ds(1, H)].reshape(PIX, C))
    sc2[...] = picked.astype(BF16).reshape(H, 16, C)
    halo_copies = [
        send(hid.at[:, pl.ds(1 + 15 * (1 - sy), 1)], hr2, halo2, 0, 0, near[0]),
        send(sc2, hc2.at[pl.ds(1, H)], halo2, 1, 1, near[1]),
        send(sc2.at[pl.ds(15 * (1 - sy), 1)], hc2.at[pl.ds(17 * sy, 1)], halo2, 2, 2, near[2]),
    ]
    for c in halo_copies:
        c.start()

    for f in range(T):
        left = jnp.concatenate([hid[f, pl.ds(dy, H)].reshape(PIX, C) for dy in range(3)], axis=1)
        direct = skip[...] * xp[f, pl.ds(2, H)].reshape(PIX, C).astype(F32)
        acc[f] = shifted(dot(left, wc2[...]), 3, C, 1) + direct

    for c in halo_copies:
        c.wait()
    first = pl.multiple_of(2 * C * (1 - sy), C)
    extra = shifted(dot(hr2[...].reshape(T * W, C), wc2[pl.ds(first, C), :]), 3, C, 1).reshape(T, W, C)
    at = pl.multiple_of(15 * W * (1 - sy), W)
    for f in range(T):
        acc[f, pl.ds(at, W), :] += extra[f]
    left = jnp.concatenate([hc2[pl.ds(dy, H)].reshape(PIX, C) for dy in range(3)], axis=1)
    first = pl.multiple_of(2 * C * (1 - sx), C)
    side = dot(left, wc2[:, pl.ds(first, C)]).reshape(H, 16, C)
    at = pl.multiple_of(8 * (1 - sx), 8)
    outer = lax.broadcasted_iota(jnp.int32, (1, 8, C), 1) == 7 * (1 - sx)
    acc4 = acc.reshape(T, H, W, C)
    for f in range(T):
        acc4[f, :, pl.ds(at, 8), :] += jnp.where(outer, side[:, f:f + 1, :], 0.0)
    for f in range(T):
        out[f] = acc[f].reshape(H, W, C).astype(BF16)


def body(frames, in_kernel, dt_weight, rates, out_kernel, skip):
    cols = lax.axis_size("tm") // ROW
    vmem = pl.BlockSpec(memory_space=pltpu.VMEM)
    hbm = pl.BlockSpec(memory_space=pl.ANY)

    def kernel(*refs):
        layer_kernel(cols, *refs)

    dma = pltpu.SemaphoreType.DMA
    chunk = (H, S)
    return pl.pallas_call(
        kernel,
        out_shape=jax.ShapeDtypeStruct(frames.shape, BF16),
        in_specs=[hbm, hbm, vmem, vmem, hbm, vmem],
        out_specs=vmem,
        scratch_shapes=[
            pltpu.VMEM((T, H + 4, W, C), BF16),
            pltpu.VMEM((5 * C, 5 * S), BF16),
            pltpu.VMEM((3 * C, 3 * C), BF16),
            pltpu.VMEM((T, 3, W, C), BF16),
            pltpu.VMEM((H + 4, 16, C), BF16),
            pltpu.VMEM((H, 16, C), BF16),
            pltpu.VMEM((T, PIX, S), F32),
            pltpu.VMEM((T, PIX, S), F32),
            pltpu.VMEM((T, PIX, S), F32),
            pltpu.VMEM((T, PIX, S), F32),
            pltpu.VMEM((T, H + 2, W, C), BF16),
            pltpu.VMEM((T, 1, W, C), BF16),
            pltpu.VMEM((H + 2, 16, C), BF16),
            pltpu.VMEM((H, 16, C), BF16),
            pltpu.VMEM((T, PIX, C), F32),
            pltpu.VMEM((ROW,) + chunk, F32),
            pltpu.VMEM((ROW,) + chunk, F32),
            pltpu.VMEM((ROW,) + chunk, F32),
            pltpu.VMEM((ROW,) + chunk, F32),
            pltpu.VMEM((cols,) + chunk, F32),
            pltpu.VMEM((cols,) + chunk, F32),
            pltpu.VMEM(chunk, F32),
            pltpu.VMEM(chunk, F32),
            pltpu.VMEM((ROW,) + chunk, F32),
            pltpu.VMEM((ROW,) + chunk, F32),
            dma,
            dma((25,)),
            dma((18,)),
            dma((2, 3)),
            dma((2, 3)),
            dma((2, ROW)),
            dma((2, ROW)),
            dma((2, cols)),
            dma((2, cols)),
            dma((2, ROW)),
        ],
        compiler_params=pltpu.CompilerParams(
            collective_id=0, has_side_effects=True, vmem_limit_bytes=48 * 1024 * 1024),
    )(frames, in_kernel.reshape(25, C, S), dt_weight, rates.reshape(1, S),
      out_kernel.reshape(9, S, C), skip.reshape(1, C))


def solution(mesh):
    return jax.shard_map(
        body,
        mesh=mesh,
        in_specs=(P("tm", "sy", "sx", None), P(), P(), P(), P(), P()),
        out_specs=P("tm", "sy", "sx", None),
        check_vma=False,
    )
```

time: 419 us -> 52.2 us (0.12)
  the two profiles are of different devices: /device:TPU:57 before, /device:TPU:1 now
where the time goes in v2:
time: 52.2 us; the launch traced here: 51.9 us
  Pallas kernels  45.6 us (87%)
  local copies, waits for them, and re-layouts  6.32 us (12%)
    pallas_call x1, Pallas kernels, body(): pl.pallas_call(kernel, out_shape=jax.ShapeDtypeStruct(frames.shape, BF16)...  45.6 us
    unnamed x13, local copies, waits for them, and re-layouts  6.32 us

profile of v2, /device:TPU:1, one launch (start us, length us, event | category | flops | bytes accessed | tf_op | source)
XLA Modules:
  0.0 51.9 jit_solution(7933722881002684517)
XLA Ops:
  0.0 0.0 copy-start
  0.0 1.4 %copy-done = bf16[5,5,256,128]{3,2,1,0:T(8,128)(2,1)S(1)} copy-done((bf16[5,5,256,128]{3,2,1,0:T(8,128)(2,1)S(1)}, bf16[5,5,256,128]{3,2,1,0:T(8,128)(2,1)}, u32[]{:S(2)}) %copy-start) | copy-done | bytes 1638424
  1.4 0.0 copy-start.1
  1.4 1.1 %copy-done.1 = bf16[3,3,128,256]{3,2,1,0:T(8,128)(2,1)S(1)} copy-done((bf16[3,3,128,256]{3,2,1,0:T(8,128)(2,1)S(1)}, bf16[3,3,128,256]{3,2,1,0:T(8,128)(2,1)}, u32[]{:S(2)}) %copy-start.1) | copy-done | bytes 589848
  2.5 0.0 copy-start.2
  2.5 1.0 %copy-done.2 = bf16[4,16,16,256]{3,2,1,0:T(8,128)(2,1)S(1)} copy-done((bf16[4,16,16,256]{3,2,1,0:T(8,128)(2,1)S(1)}, bf16[4,16,16,256]{3,2,1,0:T(8,128)(2,1)}, u32[]{:S(2)}) %copy-start.2) | copy-done | bytes 524312
  3.5 0.0 copy-start.3
  3.5 0.7 %copy-done.3 = f32[256]{0:T(256)S(1)} copy-done((f32[256]{0:T(256)S(1)}, f32[256]{0:T(256)}, u32[]{:S(2)}) %copy-start.3) | copy-done | bytes 1048
  4.2 0.0 copy-start.4
  4.2 0.7 %copy-done.4 = bf16[256]{0:T(256)(128)(2,1)S(1)} copy-done((bf16[256]{0:T(256)(128)(2,1)S(1)}, bf16[256]{0:T(256)(128)(2,1)}, u32[]{:S(2)}) %copy-start.4) | copy-done | bytes 536
  4.9 0.0 copy-start.5
  4.9 0.7 %copy-done.5 = f32[128]{0:T(128)S(1)} copy-done((f32[128]{0:T(128)S(1)}, f32[128]{0:T(128)}, u32[]{:S(2)}) %copy-start.5) | copy-done | bytes 536
  5.5 45.6 %shard_map.64 = bf16[4,16,16,256]{3,2,1,0:T(8,128)(2,1)S(1)} custom-call(bf16[4,16,16,256]{3,2,1,0:T(8,128)(2,1)S(1)} %copy-done.2, bf16[25,256,128]{2,1,0:T(8,128)(2,1)S(1)} %bitcast.4, bf16[256]{0:T(256)(128)(2,1)S(1)} %copy-done.4, f32[1,128]{1,0:T(1,128)S(1)} %bitcast.7, bf16[9,128,256]{2,1,0:T(8,128)(2,1)S(1)} %bitcast.5, f32[1,256]{1,0:T(1,128)S(1)} %bitcast.6), custom_call_target="tpu_custom_call" | custom-call | tf_op jit(solution)/shard_map/pallas_call | solution.py:265
  51.2 0.8 %copy.8 = bf16[4,16,16,256]{3,2,1,0:T(8,128)(2,1)} copy(bf16[4,16,16,256]{3,2,1,0:T(8,128)(2,1)S(1)} %shard_map.64) | data formatting | bytes 1048576
Async XLA Ops:
  0.0 1.4 %copy-start = (bf16[5,5,256,128]{3,2,1,0:T(8,128)(2,1)S(1)}, bf16[5,5,256,128]{3,2,1,0:T(8,128)(2,1)}, u32[]{:S(2)}) copy-start(bf16[5,5,256,128]{3,2,1,0:T(8,128)(2,1)} %param.7) | copy-start | bytes 4915204
  1.4 1.1 %copy-start.1 = (bf16[3,3,128,256]{3,2,1,0:T(8,128)(2,1)S(1)}, bf16[3,3,128,256]{3,2,1,0:T(8,128)(2,1)}, u32[]{:S(2)}) copy-start(bf16[3,3,128,256]{3,2,1,0:T(8,128)(2,1)} %param.10) | copy-start | bytes 1769476
  2.5 1.0 %copy-start.2 = (bf16[4,16,16,256]{3,2,1,0:T(8,128)(2,1)S(1)}, bf16[4,16,16,256]{3,2,1,0:T(8,128)(2,1)}, u32[]{:S(2)}) copy-start(bf16[4,16,16,256]{3,2,1,0:T(8,128)(2,1)} %refs_0_.1) | copy-start | bytes 1572868
  3.5 0.7 %copy-start.3 = (f32[256]{0:T(256)S(1)}, f32[256]{0:T(256)}, u32[]{:S(2)}) copy-start(f32[256]{0:T(256)} %param.11) | copy-start | bytes 3076
  4.2 0.7 %copy-start.4 = (bf16[256]{0:T(256)(128)(2,1)S(1)}, bf16[256]{0:T(256)(128)(2,1)}, u32[]{:S(2)}) copy-start(bf16[256]{0:T(256)(128)(2,1)} %refs_2_.1) | copy-start | bytes 1540
  4.9 0.7 %copy-start.5 = (f32[128]{0:T(128)S(1)}, f32[128]{0:T(128)}, u32[]{:S(2)}) copy-start(f32[128]{0:T(128)} %param.9) | copy-start | bytes 1540

commit v3 on v2

--- a/solution.py
+++ b/solution.py
@@ -40,9 +40,9 @@
 
 
 def layer_kernel(cols, frames, w1, dt, rates, w2, skip, out,
-                 xp, wc, wc2, hr, hc, sc, gain, fade, drive, loc, hid, hr2, hc2, sc2, acc,
+                 dts, spd, skp, carried, xp, wc, wc2, hr, hc, sc, gain, fade, drive, loc, hid, hr2, hc2, sc2, acc,
                  sa, sb, ra, rb, ca, cb, ta, tb, so, inc,
-                 load, wload, w2load, halo, halo2, sems_a, sems_b, sems_ca, sems_cb, sems_o):
+                 row_ready, col_ready, small, load, wload, w2load, halo, halo2, sems_a, sems_b, sems_ca, sems_cb, sems_o):
     me = lax.axis_index("tm")
     sy = lax.axis_index("sy")
     sx = lax.axis_index("sx")
@@ -50,11 +50,14 @@
     y = lax.div(me, ROW)
     base = me - r
     peers = [lax.rem(r + d, ROW) for d in ORDER]
-    columns = [lax.rem(y + d, cols) for d in (4, 3, 5, 2, 6, 1, 7) if d < cols]
     near = [{"sy": 1 - sy}, {"sx": 1 - sx}, {"sy": 1 - sy, "sx": 1 - sx}]
 
     loads = [pltpu.make_async_copy(frames, xp.at[:, pl.ds(2, H)], load)]
     loads[0].start()
+    smalls = [pltpu.make_async_copy(dt, dts, small.at[0]), pltpu.make_async_copy(rates, spd, small.at[1]),
+              pltpu.make_async_copy(skip, skp, small.at[2])]
+    for c in smalls:
+        c.start()
     wloads = []
     for i in range(25):
         wloads.append(pltpu.make_async_copy(
@@ -82,9 +85,16 @@
     hc2[17 * sy] = zrow
 
     barrier = pltpu.get_barrier_semaphore()
-    targets = near + [{"tm": base + p} for p in peers] + [{"tm": c * ROW + r} for c in columns]
-    for where in targets:
+    for where in near:
         pl.semaphore_signal(barrier, inc=1, device_id=where, device_id_type=MESH)
+    for p in range(ROW):
+        @pl.when(p > r)
+        def _(p=p):
+            pl.semaphore_signal(barrier, inc=1, device_id={"tm": base + p}, device_id_type=MESH)
+    for c in range(cols):
+        @pl.when(c > y)
+        def _(c=c):
+            pl.semaphore_signal(barrier, inc=1, device_id={"tm": c * ROW + r}, device_id_type=MESH)
 
     loads[0].wait()
     row_id = lax.broadcasted_iota(jnp.int32, (PIX, 1), 0)
@@ -103,7 +113,15 @@
             src_ref=src, dst_ref=dst, send_sem=sems.at[0, slot_out], recv_sem=sems.at[1, slot_in],
             device_id=where, device_id_type=MESH)
 
-    pl.semaphore_wait(barrier, len(targets))
+    pl.semaphore_wait(barrier, len(near) + r + y)
+    for p in range(ROW):
+        @pl.when(p < r)
+        def _(p=p):
+            pl.semaphore_signal(row_ready, inc=1, device_id={"tm": base + p}, device_id_type=MESH)
+    for c in range(cols):
+        @pl.when(c < y)
+        def _(c=c):
+            pl.semaphore_signal(col_ready, inc=1, device_id={"tm": c * ROW + r}, device_id_type=MESH)
     halo_copies = [
         send(frames.at[:, pl.ds(14 * (1 - sy), 2)], hr.at[:, pl.ds(sy, 2)], halo, 0, 0, near[0]),
         send(sc, hc.at[pl.ds(2, H)], halo, 1, 1, near[1]),
@@ -112,8 +130,10 @@
     for c in halo_copies:
         c.start()
 
-    weight = jnp.broadcast_to(dt[...].reshape(1, C), (S, C))
-    speed = rates[...]
+    for c in smalls:
+        c.wait()
+    weight = jnp.broadcast_to(dts[...].reshape(1, C), (S, C))
+    speed = spd[...]
     faded = None
     for f in range(T):
         v = lax.dot_general(xp[f, pl.ds(2, H)].reshape(PIX, C), weight, (((1,), (1,)), ((), ())),
@@ -125,8 +145,6 @@
         faded = decay if f == 0 else faded * decay
         fade[f] = faded
     sa[...] = faded.reshape(ROW, H, S)
-    for p in peers:
-        send(sa.at[p], ra.at[r], sems_a, p, r, {"tm": base + p}).start()
     ra[r] = sa[r]
 
     for c in wloads:
@@ -134,6 +152,11 @@
     for f in range(T):
         left = jnp.concatenate([xp[f, pl.ds(dy, H)].reshape(PIX, C) for dy in range(5)], axis=1)
         drive[f] = shifted(dot(left, wc[...]), 5, S, 2)
+    @pl.when(r < ROW - 1)
+    def _():
+        pl.semaphore_wait(row_ready, ROW - 1 - r)
+    for p in peers:
+        send(sa.at[p], ra.at[r], sems_a, p, r, {"tm": base + p}).start()
 
     for c in halo_copies:
         c.wait()
@@ -175,8 +198,13 @@
     for k in range(1, ROW):
         total_a = total_a * ra[k]
     ta[...] = total_a
-    for c in columns:
-        send(ta, ca.at[y], sems_ca, c, y, {"tm": c * ROW + r}).start()
+    @pl.when(y < cols - 1)
+    def _():
+        pl.semaphore_wait(col_ready, cols - 1 - y)
+    for c in range(cols):
+        @pl.when(c > y)
+        def _(c=c):
+            send(ta, ca.at[y], sems_ca, c, y, {"tm": c * ROW + r}).start()
     for c in w2loads:
         c.wait()
 
@@ -186,17 +214,18 @@
     for k in range(1, ROW):
         total_b = ra[k] * total_b + rb[k]
     tb[...] = total_b
-    for c in columns:
-        send(tb, cb.at[y], sems_cb, c, y, {"tm": c * ROW + r}).start()
-    for c in columns:
-        send(ta, ca.at[c], sems_ca, c, c, {"tm": c * ROW + r}).wait()
-    for c in columns:
-        send(tb, cb.at[c], sems_cb, c, c, {"tm": c * ROW + r}).wait()
-    ca[y] = total_a
-    cb[y] = total_b
-    carry = jnp.zeros_like(total_b)
-    for c in range(cols):
-        carry = jnp.where(c < y, ca[c] * carry + cb[c], carry)
+    for c in range(cols):
+        @pl.when(c > y)
+        def _(c=c):
+            send(tb, cb.at[y], sems_cb, c, y, {"tm": c * ROW + r}).start()
+    carried[...] = jnp.zeros_like(total_b)
+    for c in range(cols):
+        @pl.when(c < y)
+        def _(c=c):
+            send(ta, ca.at[c], sems_ca, c, c, {"tm": c * ROW + r}).wait_recv()
+            send(tb, cb.at[c], sems_cb, c, c, {"tm": c * ROW + r}).wait_recv()
+            carried[...] = ca[c] * carried[...] + cb[c]
+    carry = carried[...]
     so[0] = carry
     for k in range(ROW - 1):
         carry = ra[k] * carry + rb[k]
@@ -206,6 +235,12 @@
     inc[r] = so[r]
     for p in peers:
         send(so.at[p], inc.at[p], sems_o, p, p, {"tm": base + p}).wait()
+
+    for c in range(cols):
+        @pl.when(c > y)
+        def _(c=c):
+            send(ta, ca.at[y], sems_ca, c, y, {"tm": c * ROW + r}).wait_send()
+            send(tb, cb.at[y], sems_cb, c, y, {"tm": c * ROW + r}).wait_send()
 
     before = inc[...].reshape(PIX, S)
     for f in range(T):
@@ -230,7 +265,7 @@
 
     for f in range(T):
         left = jnp.concatenate([hid[f, pl.ds(dy, H)].reshape(PIX, C) for dy in range(3)], axis=1)
-        direct = skip[...] * xp[f, pl.ds(2, H)].reshape(PIX, C).astype(F32)
+        direct = skp[...] * xp[f, pl.ds(2, H)].reshape(PIX, C).astype(F32)
         acc[f] = shifted(dot(left, wc2[...]), 3, C, 1) + direct
 
     for c in halo_copies:
@@ -255,7 +290,7 @@
 def body(frames, in_kernel, dt_weight, rates, out_kernel, skip):
     cols = lax.axis_size("tm") // ROW
     vmem = pl.BlockSpec(memory_space=pltpu.VMEM)
-    hbm = pl.BlockSpec(memory_space=pl.ANY)
+    hbm = pl.BlockSpec(memory_space=pltpu.HBM)
 
     def kernel(*refs):
         layer_kernel(cols, *refs)
@@ -265,9 +300,13 @@
     return pl.pallas_call(
         kernel,
         out_shape=jax.ShapeDtypeStruct(frames.shape, BF16),
-        in_specs=[hbm, hbm, vmem, vmem, hbm, vmem],
+        in_specs=[hbm] * 6,
         out_specs=vmem,
         scratch_shapes=[
+            pltpu.VMEM((C,), BF16),
+            pltpu.VMEM((1, S), F32),
+            pltpu.VMEM((1, C), F32),
+            pltpu.VMEM(chunk, F32),
             pltpu.VMEM((T, H + 4, W, C), BF16),
             pltpu.VMEM((5 * C, 5 * S), BF16),
             pltpu.VMEM((3 * C, 3 * C), BF16),
@@ -293,6 +332,9 @@
             pltpu.VMEM(chunk, F32),
             pltpu.VMEM((ROW,) + chunk, F32),
             pltpu.VMEM((ROW,) + chunk, F32),
+            pltpu.SemaphoreType.REGULAR,
+            pltpu.SemaphoreType.REGULAR,
+            dma((3,)),
             dma,
             dma((25,)),
             dma((18,)),
@@ -305,7 +347,7 @@
             dma((2, ROW)),
         ],
         compiler_params=pltpu.CompilerParams(
-            collective_id=0, has_side_effects=True, vmem_limit_bytes=48 * 1024 * 1024),
+            collective_id=0, has_side_effects=True, vmem_limit_bytes=67_000_000),
     )(frames, in_kernel.reshape(25, C, S), dt_weight, rates.reshape(1, S),
       out_kernel.reshape(9, S, C), skip.reshape(1, C))
 

time: 52.2 us -> 44.5 us (0.85)
  the two profiles are of different devices: /device:TPU:1 before, /device:TPU:57 now
where the time goes in v3:
time: 44.5 us; the launch traced here: 43.9 us
  Pallas kernels  42.1 us (95%)
  local copies, waits for them, and re-layouts  1.87 us (4%)
    pallas_call x1, Pallas kernels, body(): pl.pallas_call(kernel, out_shape=jax.ShapeDtypeStruct(frames.shape, BF16)...  42.1 us
    unnamed x1, local copies, waits for them, and re-layouts  1.87 us

profile of v3, /device:TPU:57, one launch (start us, length us, event | category | flops | bytes accessed | tf_op | source)
XLA Modules:
  0.0 43.9 jit_solution(5276178572788530509)
XLA Ops:
  0.0 42.1 %shard_map.64 = bf16[4,16,16,256]{3,2,1,0:T(8,128)(2,1)} custom-call(bf16[4,16,16,256]{3,2,1,0:T(8,128)(2,1)} %refs_0_.1, bf16[25,256,128]{2,1,0:T(8,128)(2,1)} %bitcast.4, bf16[256]{0:T(256)(128)(2,1)} %refs_2_.1, f32[1,128]{1,0:T(1,128)} %bitcast.7, bf16[9,128,256]{2,1,0:T(8,128)(2,1)} %bitcast.5, f32[1,256]{1,0:T(1,128)} %bitcast.6), custom_call_target="tpu_custom_call" | custom-call | tf_op jit(solution)/shard_map/pallas_call | solution.py:300
  42.1 1.9 %copy.8 = bf16[4,16,16,256]{3,2,1,0:T(8,128)(2,1)} copy(bf16[4,16,16,256]{3,2,1,0:T(8,128)(2,1)} %shard_map.64) | data formatting | bytes 1048576

commit v4 on v3

--- a/solution.py
+++ b/solution.py
@@ -40,9 +40,9 @@
 
 
 def layer_kernel(cols, frames, w1, dt, rates, w2, skip, out,
-                 dts, spd, skp, carried, xp, wc, wc2, hr, hc, sc, gain, fade, drive, loc, hid, hr2, hc2, sc2, acc,
+                 dts, spd, skp, carried, xp, wc, wc2, hr, hc, sc, gain, fade, drive, loc, hid, hr2, hc2, acc, er, ec, ner, nec, se, ie, ir,
                  sa, sb, ra, rb, ca, cb, ta, tb, so, inc,
-                 row_ready, col_ready, small, load, wload, w2load, halo, halo2, sems_a, sems_b, sems_ca, sems_cb, sems_o):
+                 row_ready, col_ready, tile_ready, small, load, wload, w2load, halo, halo2, sems_a, sems_b, sems_ca, sems_cb, sems_o, sems_e, sems_r, sems_c):
     me = lax.axis_index("tm")
     sy = lax.axis_index("sy")
     sx = lax.axis_index("sx")
@@ -81,8 +81,9 @@
         hid[f, 0] = zrow
         hid[f, 17] = zrow
     for row in range(2):
-        hc[18 * sy + row] = zrow
-    hc2[17 * sy] = zrow
+        hc[18 * sy + row] = zrow[:8]
+    nec[17 * sy] = jnp.zeros((8, S), F32)
+    ie[17 * sy] = jnp.zeros((1, S), F32)
 
     barrier = pltpu.get_barrier_semaphore()
     for where in near:
@@ -97,16 +98,16 @@
             pl.semaphore_signal(barrier, inc=1, device_id={"tm": c * ROW + r}, device_id_type=MESH)
 
     loads[0].wait()
-    row_id = lax.broadcasted_iota(jnp.int32, (PIX, 1), 0)
-    slot = lax.rem(row_id, 16)
+    row_id = lax.broadcasted_iota(jnp.int32, (8 * H, 1), 0)
+    slot = lax.rem(row_id, 8)
     edge = jnp.where(sx == 0, 15 - slot // 4, slot // 4)
-    target = jnp.where(slot < 8, lax.rem(slot, 4) * PIX + (row_id // 16) * W + edge, -1)
-    lane = lax.broadcasted_iota(jnp.int32, (PIX, PIX), 1)
-    picked = jnp.zeros((PIX, C), F32)
+    target = lax.rem(slot, 4) * PIX + (row_id // 8) * W + edge
+    lane = lax.broadcasted_iota(jnp.int32, (8 * H, PIX), 1)
+    picked = jnp.zeros((8 * H, C), F32)
     for f in range(T):
         pick = jnp.where(lane + f * PIX == target, 1.0, 0.0).astype(BF16)
         picked = picked + dot(pick, xp[f, pl.ds(2, H)].reshape(PIX, C))
-    sc[...] = picked.astype(BF16).reshape(H, 16, C)
+    sc[...] = picked.astype(BF16).reshape(H, 8, C)
 
     def send(src, dst, sems, slot_out, slot_in, where):
         return pltpu.make_async_remote_copy(
@@ -166,9 +167,9 @@
     at = pl.multiple_of(14 * W * (1 - sy), 2 * W)
     for f in range(T):
         drive[f, pl.ds(at, 2 * W), :] += extra[f]
-    left = jnp.concatenate([hc[pl.ds(dy, H)].reshape(PIX, C) for dy in range(5)], axis=1)
+    left = jnp.concatenate([hc[pl.ds(dy, H)].reshape(8 * H, C) for dy in range(5)], axis=1)
     first = pl.multiple_of(3 * S * (1 - sx), S)
-    side = dot(left, wc[:, pl.ds(first, 2 * S)]).reshape(H, 16, 2 * S)
+    side = dot(left, wc[:, pl.ds(first, 2 * S)]).reshape(H, 8, 2 * S)
     close = jnp.where(sx == 0, side[:, :, :S], side[:, :, S:])
     far = jnp.where(sx == 0, side[:, :, S:], side[:, :, :S])
     lane8 = lax.broadcasted_iota(jnp.int32, (1, 8, S), 1)
@@ -191,6 +192,27 @@
     for p in peers:
         send(sb.at[p], rb.at[r], sems_b, p, r, {"tm": base + p}).start()
     rb[r] = sb[r]
+
+    for where in near:
+        pl.semaphore_signal(tile_ready, inc=1, device_id=where, device_id_type=MESH)
+    edge_row = pl.multiple_of(15 * W * (1 - sy), W)
+    edge_x = 15 * (1 - sx)
+    at_edge = lax.broadcasted_iota(jnp.int32, (1, W, S), 1) == edge_x
+    ends = []
+    for ref in (loc, fade):
+        for f in range(T):
+            ends.append(jnp.sum(jnp.where(at_edge, ref[f].reshape(H, W, S), 0.0), axis=1, keepdims=True))
+    ec[...] = jnp.concatenate(ends, axis=1)
+    for f in range(T):
+        er[f] = loc[f, pl.ds(edge_row, W), :]
+        er[T + f] = fade[f, pl.ds(edge_row, W), :]
+    edge_copies = [
+        send(er, ner, halo2, 0, 0, near[0]),
+        send(ec, nec.at[pl.ds(1, H)], halo2, 1, 1, near[1]),
+        send(ec.at[pl.ds(15 * (1 - sy), 1)], nec.at[pl.ds(17 * sy, 1)], halo2, 2, 2, near[2]),
+    ]
+    for c in edge_copies:
+        c.start()
 
     for p in peers:
         send(sa.at[p], ra.at[p], sems_a, p, p, {"tm": base + p}).wait()
@@ -233,6 +255,28 @@
     for p in peers:
         send(so.at[p], inc.at[r], sems_o, p, r, {"tm": base + p}).start()
     inc[r] = so[r]
+    for k in range(ROW):
+        se[k] = jnp.sum(jnp.where(at_edge[0], so[k], 0.0), axis=0, keepdims=True)
+    pl.semaphore_wait(tile_ready, len(near))
+    everyone = [r] + peers
+
+    def to_column(p):
+        return send(se.at[pl.ds(p, 1)], ie.at[pl.ds(1 + r, 1)], sems_e, p, r, {"tm": base + p, "sx": 1 - sx})
+
+    def to_row(p):
+        return send(so.at[p], ir, sems_r, p, 0, {"tm": base + p, "sy": 1 - sy})
+
+    def to_corner(p):
+        return send(se.at[pl.ds(p, 1)], ie.at[pl.ds(17 * sy, 1)], sems_c, p, 0,
+                    {"tm": base + p, "sy": 1 - sy, "sx": 1 - sx})
+
+    @pl.when(r == 15 * (1 - sy))
+    def _():
+        for p in everyone:
+            to_row(p).start()
+            to_corner(p).start()
+    for p in everyone:
+        to_column(p).start()
     for p in peers:
         send(so.at[p], inc.at[p], sems_o, p, p, {"tm": base + p}).wait()
 
@@ -248,36 +292,42 @@
         high = state.astype(BF16)
         low = (state - high.astype(F32)).astype(BF16)
         hid[f, pl.ds(1, H)] = jnp.concatenate([high, low], axis=1).reshape(H, W, C)
-    edge = 15 * (1 - sx)
-    target = jnp.where(slot < 4, slot * PIX + (row_id // 16) * W + edge, -1)
-    picked = jnp.zeros((PIX, C), F32)
-    for f in range(T):
-        pick = jnp.where(lane + f * PIX == target, 1.0, 0.0).astype(BF16)
-        picked = picked + dot(pick, hid[f, pl.ds(1, H)].reshape(PIX, C))
-    sc2[...] = picked.astype(BF16).reshape(H, 16, C)
-    halo_copies = [
-        send(hid.at[:, pl.ds(1 + 15 * (1 - sy), 1)], hr2, halo2, 0, 0, near[0]),
-        send(sc2, hc2.at[pl.ds(1, H)], halo2, 1, 1, near[1]),
-        send(sc2.at[pl.ds(15 * (1 - sy), 1)], hc2.at[pl.ds(17 * sy, 1)], halo2, 2, 2, near[2]),
-    ]
-    for c in halo_copies:
-        c.start()
 
     for f in range(T):
         left = jnp.concatenate([hid[f, pl.ds(dy, H)].reshape(PIX, C) for dy in range(3)], axis=1)
         direct = skp[...] * xp[f, pl.ds(2, H)].reshape(PIX, C).astype(F32)
         acc[f] = shifted(dot(left, wc2[...]), 3, C, 1) + direct
 
-    for c in halo_copies:
+    for c in edge_copies:
         c.wait()
+    for p in everyone:
+        send(se.at[pl.ds(p, 1)], ie.at[pl.ds(1 + p, 1)], sems_e, p, p, {"tm": base + p, "sx": 1 - sx}).wait()
+    to_row(r).wait_recv()
+    to_corner(r).wait_recv()
+
+    @pl.when(r == 15 * (1 - sy))
+    def _():
+        for p in everyone:
+            to_row(p).wait_send()
+            to_corner(p).wait_send()
+    state = ner[pl.ds(0, T)] + ner[pl.ds(T, T)] * ir[...].reshape(1, W, S)
+    high = state.astype(BF16)
+    hr2[...] = jnp.concatenate([high, (state - high.astype(F32)).astype(BF16)], axis=2)
+    both = nec[...]
+    state = both[:, :T] + both[:, T:] * ie[...]
+    there = lax.broadcasted_iota(jnp.int32, (H + 2, 1, 1), 0) != 17 * sy
+    state = jnp.where(there, state, 0.0)
+    state = jnp.concatenate([state, jnp.zeros_like(state)], axis=1)
+    high = state.astype(BF16)
+    hc2[...] = jnp.concatenate([high, (state - high.astype(F32)).astype(BF16)], axis=2)
     first = pl.multiple_of(2 * C * (1 - sy), C)
     extra = shifted(dot(hr2[...].reshape(T * W, C), wc2[pl.ds(first, C), :]), 3, C, 1).reshape(T, W, C)
     at = pl.multiple_of(15 * W * (1 - sy), W)
     for f in range(T):
         acc[f, pl.ds(at, W), :] += extra[f]
-    left = jnp.concatenate([hc2[pl.ds(dy, H)].reshape(PIX, C) for dy in range(3)], axis=1)
+    left = jnp.concatenate([hc2[pl.ds(dy, H)].reshape(8 * H, C) for dy in range(3)], axis=1)
     first = pl.multiple_of(2 * C * (1 - sx), C)
-    side = dot(left, wc2[:, pl.ds(first, C)]).reshape(H, 16, C)
+    side = dot(left, wc2[:, pl.ds(first, C)]).reshape(H, 8, C)
     at = pl.multiple_of(8 * (1 - sx), 8)
     outer = lax.broadcasted_iota(jnp.int32, (1, 8, C), 1) == 7 * (1 - sx)
     acc4 = acc.reshape(T, H, W, C)
@@ -311,17 +361,23 @@
             pltpu.VMEM((5 * C, 5 * S), BF16),
             pltpu.VMEM((3 * C, 3 * C), BF16),
             pltpu.VMEM((T, 3, W, C), BF16),
-            pltpu.VMEM((H + 4, 16, C), BF16),
-            pltpu.VMEM((H, 16, C), BF16),
+            pltpu.VMEM((H + 4, 8, C), BF16),
+            pltpu.VMEM((H, 8, C), BF16),
             pltpu.VMEM((T, PIX, S), F32),
             pltpu.VMEM((T, PIX, S), F32),
             pltpu.VMEM((T, PIX, S), F32),
             pltpu.VMEM((T, PIX, S), F32),
             pltpu.VMEM((T, H + 2, W, C), BF16),
-            pltpu.VMEM((T, 1, W, C), BF16),
-            pltpu.VMEM((H + 2, 16, C), BF16),
-            pltpu.VMEM((H, 16, C), BF16),
+            pltpu.VMEM((T, W, C), BF16),
+            pltpu.VMEM((H + 2, 8, C), BF16),
             pltpu.VMEM((T, PIX, C), F32),
+            pltpu.VMEM((2 * T, W, S), F32),
+            pltpu.VMEM((H, 2 * T, S), F32),
+            pltpu.VMEM((2 * T, W, S), F32),
+            pltpu.VMEM((H + 2, 2 * T, S), F32),
+            pltpu.VMEM((ROW, 1, S), F32),
+            pltpu.VMEM((H + 2, 1, S), F32),
+            pltpu.VMEM(chunk, F32),
             pltpu.VMEM((ROW,) + chunk, F32),
             pltpu.VMEM((ROW,) + chunk, F32),
             pltpu.VMEM((ROW,) + chunk, F32),
@@ -332,6 +388,7 @@
             pltpu.VMEM(chunk, F32),
             pltpu.VMEM((ROW,) + chunk, F32),
             pltpu.VMEM((ROW,) + chunk, F32),
+            pltpu.SemaphoreType.REGULAR,
             pltpu.SemaphoreType.REGULAR,
             pltpu.SemaphoreType.REGULAR,
             dma((3,)),
@@ -345,6 +402,9 @@
             dma((2, cols)),
             dma((2, cols)),
             dma((2, ROW)),
+            dma((2, ROW)),
+            dma((2, ROW)),
+            dma((2, ROW)),
         ],
         compiler_params=pltpu.CompilerParams(
             collective_id=0, has_side_effects=True, vmem_limit_bytes=67_000_000),

time: 44.5 us -> 40.9 us (0.919)
  Pallas kernels: 42.1 us -> 38.9 us
    pallas_call x1, Pallas kernels: 42.1 us -> 38.9 us  [body(): pl.pallas_call(kernel, out_shape=jax.ShapeDtypeStruct(frames.shape, BF16)...]
where the time goes in v4:
time: 40.9 us; the launch traced here: 40.8 us
  Pallas kernels  38.9 us (95%)
  local copies, waits for them, and re-layouts  1.87 us (5%)
    pallas_call x1, Pallas kernels, body(): pl.pallas_call(kernel, out_shape=jax.ShapeDtypeStruct(frames.shape, BF16)...  38.9 us
    unnamed x1, local copies, waits for them, and re-layouts  1.87 us

profile of v4, /device:TPU:57, one launch (start us, length us, event | category | flops | bytes accessed | tf_op | source)
XLA Modules:
  0.0 40.8 jit_solution(7937811719543618567)
XLA Ops:
  0.0 38.9 %shard_map.64 = bf16[4,16,16,256]{3,2,1,0:T(8,128)(2,1)} custom-call(bf16[4,16,16,256]{3,2,1,0:T(8,128)(2,1)} %refs_0_.1, bf16[25,256,128]{2,1,0:T(8,128)(2,1)} %bitcast.4, bf16[256]{0:T(256)(128)(2,1)} %refs_2_.1, f32[1,128]{1,0:T(1,128)} %bitcast.7, bf16[9,128,256]{2,1,0:T(8,128)(2,1)} %bitcast.5, f32[1,256]{1,0:T(1,128)} %bitcast.6), custom_call_target="tpu_custom_call" | custom-call | tf_op jit(solution)/shard_map/pallas_call | solution.py:350
  38.9 1.9 %copy.8 = bf16[4,16,16,256]{3,2,1,0:T(8,128)(2,1)} copy(bf16[4,16,16,256]{3,2,1,0:T(8,128)(2,1)} %shard_map.64) | data formatting | bytes 1048576

commit v5 on v4

--- a/solution.py
+++ b/solution.py
@@ -40,9 +40,9 @@
 
 
 def layer_kernel(cols, frames, w1, dt, rates, w2, skip, out,
-                 dts, spd, skp, carried, xp, wc, wc2, hr, hc, sc, gain, fade, drive, loc, hid, hr2, hc2, acc, er, ec, ner, nec, se, ie, ir,
+                 dts, spd, skp, carried, xp, wc, wc2, hr, hc, sc, gain, fade, keep, loc, hid, hr2, hc2, acc, done, er, ec, ner, nec, se, ie, ir,
                  sa, sb, ra, rb, ca, cb, ta, tb, so, inc,
-                 row_ready, col_ready, tile_ready, small, load, wload, w2load, halo, halo2, sems_a, sems_b, sems_ca, sems_cb, sems_o, sems_e, sems_r, sems_c):
+                 row_ready, col_ready, tile_ready, small, store, load, wload, w2load, halo, halo2, sems_a, sems_b, sems_ca, sems_cb, sems_o, sems_e, sems_r, sems_c):
     me = lax.axis_index("tm")
     sy = lax.axis_index("sy")
     sx = lax.axis_index("sx")
@@ -51,6 +51,30 @@
     base = me - r
     peers = [lax.rem(r + d, ROW) for d in ORDER]
     near = [{"sy": 1 - sy}, {"sx": 1 - sx}, {"sy": 1 - sy, "sx": 1 - sx}]
+
+    zrow = jnp.zeros((W, C), BF16)
+    for f in range(T):
+        for row in (0, 1, 18, 19):
+            xp[f, row] = zrow
+        hr[f, 2 * sy] = zrow
+        hid[f, 0] = zrow
+        hid[f, 17] = zrow
+    for row in range(2):
+        hc[18 * sy + row] = zrow[:8]
+    nec[17 * sy] = jnp.zeros((8, S), F32)
+    ie[17 * sy] = jnp.zeros((1, S), F32)
+
+    barrier = pltpu.get_barrier_semaphore()
+    for where in near:
+        pl.semaphore_signal(barrier, inc=1, device_id=where, device_id_type=MESH)
+    for p in range(ROW):
+        @pl.when(p > r)
+        def _(p=p):
+            pl.semaphore_signal(barrier, inc=1, device_id={"tm": base + p}, device_id_type=MESH)
+    for c in range(cols):
+        @pl.when(c > y)
+        def _(c=c):
+            pl.semaphore_signal(barrier, inc=1, device_id={"tm": c * ROW + r}, device_id_type=MESH)
 
     loads = [pltpu.make_async_copy(frames, xp.at[:, pl.ds(2, H)], load)]
     loads[0].start()
@@ -62,40 +86,31 @@
     for i in range(25):
         wloads.append(pltpu.make_async_copy(
             w1.at[i], wc.at[pl.ds((i // 5) * C, C), pl.ds((i % 5) * S, S)], wload.at[i]))
-    for c in wloads:
-        c.start()
     w2loads = []
     for i in range(9):
         for half in range(2):
             w2loads.append(pltpu.make_async_copy(
                 w2.at[i], wc2.at[pl.ds((i // 3) * C + half * S, S), pl.ds((i % 3) * C, C)],
                 w2load.at[2 * i + half]))
-    for c in w2loads:
+
+    def send(src, dst, sems, slot_out, slot_in, where):
+        return pltpu.make_async_remote_copy(
+            src_ref=src, dst_ref=dst, send_sem=sems.at[0, slot_out], recv_sem=sems.at[1, slot_in],
+            device_id=where, device_id_type=MESH)
+
+    pl.semaphore_wait(barrier, len(near) + r + y)
+    for p in range(ROW):
+        @pl.when(p < r)
+        def _(p=p):
+            pl.semaphore_signal(row_ready, inc=1, device_id={"tm": base + p}, device_id_type=MESH)
+    for c in range(cols):
+        @pl.when(c < y)
+        def _(c=c):
+            pl.semaphore_signal(col_ready, inc=1, device_id={"tm": c * ROW + r}, device_id_type=MESH)
+    halo_copies = [send(frames.at[:, pl.ds(14 * (1 - sy), 2)], hr.at[:, pl.ds(sy, 2)], halo, 0, 0, near[0])]
+    halo_copies[0].start()
+    for c in wloads:
         c.start()
-
-    zrow = jnp.zeros((W, C), BF16)
-    for f in range(T):
-        for row in (0, 1, 18, 19):
-            xp[f, row] = zrow
-        hr[f, 2 * sy] = zrow
-        hid[f, 0] = zrow
-        hid[f, 17] = zrow
-    for row in range(2):
-        hc[18 * sy + row] = zrow[:8]
-    nec[17 * sy] = jnp.zeros((8, S), F32)
-    ie[17 * sy] = jnp.zeros((1, S), F32)
-
-    barrier = pltpu.get_barrier_semaphore()
-    for where in near:
-        pl.semaphore_signal(barrier, inc=1, device_id=where, device_id_type=MESH)
-    for p in range(ROW):
-        @pl.when(p > r)
-        def _(p=p):
-            pl.semaphore_signal(barrier, inc=1, device_id={"tm": base + p}, device_id_type=MESH)
-    for c in range(cols):
-        @pl.when(c > y)
-        def _(c=c):
-            pl.semaphore_signal(barrier, inc=1, device_id={"tm": c * ROW + r}, device_id_type=MESH)
 
     loads[0].wait()
     row_id = lax.broadcasted_iota(jnp.int32, (8 * H, 1), 0)
@@ -109,26 +124,11 @@
         picked = picked + dot(pick, xp[f, pl.ds(2, H)].reshape(PIX, C))
     sc[...] = picked.astype(BF16).reshape(H, 8, C)
 
-    def send(src, dst, sems, slot_out, slot_in, where):
-        return pltpu.make_async_remote_copy(
-            src_ref=src, dst_ref=dst, send_sem=sems.at[0, slot_out], recv_sem=sems.at[1, slot_in],
-            device_id=where, device_id_type=MESH)
-
-    pl.semaphore_wait(barrier, len(near) + r + y)
-    for p in range(ROW):
-        @pl.when(p < r)
-        def _(p=p):
-            pl.semaphore_signal(row_ready, inc=1, device_id={"tm": base + p}, device_id_type=MESH)
-    for c in range(cols):
-        @pl.when(c < y)
-        def _(c=c):
-            pl.semaphore_signal(col_ready, inc=1, device_id={"tm": c * ROW + r}, device_id_type=MESH)
-    halo_copies = [
-        send(frames.at[:, pl.ds(14 * (1 - sy), 2)], hr.at[:, pl.ds(sy, 2)], halo, 0, 0, near[0]),
+    halo_copies += [
         send(sc, hc.at[pl.ds(2, H)], halo, 1, 1, near[1]),
         send(sc.at[pl.ds(14 * (1 - sy), 2)], hc.at[pl.ds(18 * sy, 2)], halo, 2, 2, near[2]),
     ]
-    for c in halo_copies:
+    for c in halo_copies[1:]:
         c.start()
 
     for c in smalls:
@@ -142,31 +142,48 @@
         scaled = (jnp.maximum(v, 0.0) + jnp.log1p(jnp.exp(-jnp.abs(v)))) * speed
         decay = jnp.exp(-scaled)
         gain[f] = jnp.sqrt(one_minus_exp(2.0 * scaled))
-        loc[f] = decay
+        keep[f] = decay
         faded = decay if f == 0 else faded * decay
         fade[f] = faded
     sa[...] = faded.reshape(ROW, H, S)
     ra[r] = sa[r]
 
+    def send_decays():
+        @pl.when(r < ROW - 1)
+        def _():
+            pl.semaphore_wait(row_ready, ROW - 1 - r)
+        for p in peers:
+            send(sa.at[p], ra.at[r], sems_a, p, r, {"tm": base + p}).start()
+
+    @pl.when(r >= ROW // 2)
+    def _():
+        send_decays()
+
     for c in wloads:
         c.wait()
     for f in range(T):
         left = jnp.concatenate([xp[f, pl.ds(dy, H)].reshape(PIX, C) for dy in range(5)], axis=1)
-        drive[f] = shifted(dot(left, wc[...]), 5, S, 2)
-    @pl.when(r < ROW - 1)
+        fresh = gain[f] * shifted(dot(left, wc[...]), 5, S, 2)
+        loc[f] = fresh if f == 0 else fresh + keep[f] * loc[f - 1]
+
+    for c in w2loads:
+        c.start()
+
+    @pl.when(r < ROW // 2)
     def _():
-        pl.semaphore_wait(row_ready, ROW - 1 - r)
-    for p in peers:
-        send(sa.at[p], ra.at[r], sems_a, p, r, {"tm": base + p}).start()
+        send_decays()
 
     for c in halo_copies:
         c.wait()
     left = jnp.concatenate([hr[:, pl.ds(k, 2)].reshape(T * 2 * W, C) for k in range(2)], axis=1)
     first = pl.multiple_of(3 * C * (1 - sy), C)
     extra = shifted(dot(left, wc[pl.ds(first, 2 * C), :]), 5, S, 2).reshape(T, 2 * W, S)
-    at = pl.multiple_of(14 * W * (1 - sy), 2 * W)
-    for f in range(T):
-        drive[f, pl.ds(at, 2 * W), :] += extra[f]
+    at = pl.ds(pl.multiple_of(14 * W * (1 - sy), 2 * W), 2 * W)
+    more = None
+    for f in range(T):
+        fresh = gain[f, at, :] * extra[f]
+        more = fresh if f == 0 else fresh + keep[f, at, :] * more
+        loc[f, at, :] += more
     left = jnp.concatenate([hc[pl.ds(dy, H)].reshape(8 * H, C) for dy in range(5)], axis=1)
     first = pl.multiple_of(3 * S * (1 - sx), S)
     side = dot(left, wc[:, pl.ds(first, 2 * S)]).reshape(H, 8, 2 * S)
@@ -175,20 +192,15 @@
     lane8 = lax.broadcasted_iota(jnp.int32, (1, 8, S), 1)
     outer = lane8 == 7 * (1 - sx)
     inner = lane8 == 5 * (1 - sx) + 1
-    at = pl.multiple_of(8 * (1 - sx), 8)
-    drive4 = drive.reshape(T, H, W, S)
+    at = pl.ds(pl.multiple_of(8 * (1 - sx), 8), 8)
+    gain4, keep4, loc4 = (ref.reshape(T, H, W, S) for ref in (gain, keep, loc))
     for f in range(T):
         add = jnp.where(outer, close[:, f:f + 1, :] + far[:, 4 + f:5 + f, :], 0.0)
         add = add + jnp.where(inner, far[:, f:f + 1, :], 0.0)
-        drive4[f, :, pl.ds(at, 8), :] += add
-
-    state = gain[0] * drive[0]
-    for f in range(1, T):
-        decay = loc[f]
-        loc[f - 1] = state
-        state = decay * state + gain[f] * drive[f]
-    loc[T - 1] = state
-    sb[...] = state.reshape(ROW, H, S)
+        fresh = gain4[f, :, at, :] * add
+        more = fresh if f == 0 else fresh + keep4[f, :, at, :] * more
+        loc4[f, :, at, :] += more
+    sb[...] = loc[T - 1].reshape(ROW, H, S)
     for p in peers:
         send(sb.at[p], rb.at[r], sems_b, p, r, {"tm": base + p}).start()
     rb[r] = sb[r]
@@ -333,13 +345,17 @@
     acc4 = acc.reshape(T, H, W, C)
     for f in range(T):
         acc4[f, :, pl.ds(at, 8), :] += jnp.where(outer, side[:, f:f + 1, :], 0.0)
-    for f in range(T):
-        out[f] = acc[f].reshape(H, W, C).astype(BF16)
+    stores = []
+    for f in range(T):
+        done[f] = acc[f].reshape(H, W, C).astype(BF16)
+        stores.append(pltpu.make_async_copy(done.at[f], out.at[f], store.at[f]))
+        stores[f].start()
+    for c in stores:
+        c.wait()
 
 
 def body(frames, in_kernel, dt_weight, rates, out_kernel, skip):
     cols = lax.axis_size("tm") // ROW
-    vmem = pl.BlockSpec(memory_space=pltpu.VMEM)
     hbm = pl.BlockSpec(memory_space=pltpu.HBM)
 
     def kernel(*refs):
@@ -351,7 +367,7 @@
         kernel,
         out_shape=jax.ShapeDtypeStruct(frames.shape, BF16),
         in_specs=[hbm] * 6,
-        out_specs=vmem,
+        out_specs=hbm,
         scratch_shapes=[
             pltpu.VMEM((C,), BF16),
             pltpu.VMEM((1, S), F32),
@@ -371,6 +387,7 @@
             pltpu.VMEM((T, W, C), BF16),
             pltpu.VMEM((H + 2, 8, C), BF16),
             pltpu.VMEM((T, PIX, C), F32),
+            pltpu.VMEM((T, H, W, C), BF16),
             pltpu.VMEM((2 * T, W, S), F32),
             pltpu.VMEM((H, 2 * T, S), F32),
             pltpu.VMEM((2 * T, W, S), F32),
@@ -392,6 +409,7 @@
             pltpu.SemaphoreType.REGULAR,
             pltpu.SemaphoreType.REGULAR,
             dma((3,)),
+            dma((T,)),
             dma,
             dma((25,)),
             dma((18,)),

time: 40.9 us -> 40.6 us (level)
  no operation moved by 1% of the time
where the time goes in v5:
time: 40.6 us; the launch traced here: 40.4 us
  Pallas kernels  38.6 us (95%)
  local copies, waits for them, and re-layouts  1.87 us (5%)
    pallas_call x1, Pallas kernels, body(): pl.pallas_call(kernel, out_shape=jax.ShapeDtypeStruct(frames.shape, BF16)...  38.6 us
    unnamed x1, local copies, waits for them, and re-layouts  1.87 us

profile of v5, /device:TPU:57, one launch (start us, length us, event | category | flops | bytes accessed | tf_op | source)
XLA Modules:
  0.0 40.4 jit_solution(3186969185837452947)
XLA Ops:
  0.0 38.6 %shard_map.64 = bf16[4,16,16,256]{3,2,1,0:T(8,128)(2,1)} custom-call(bf16[4,16,16,256]{3,2,1,0:T(8,128)(2,1)} %refs_0_.1, bf16[25,256,128]{2,1,0:T(8,128)(2,1)} %bitcast.4, bf16[256]{0:T(256)(128)(2,1)} %refs_2_.1, f32[1,128]{1,0:T(1,128)} %bitcast.7, bf16[9,128,256]{2,1,0:T(8,128)(2,1)} %bitcast.5, f32[1,256]{1,0:T(1,128)} %bitcast.6), custom_call_target="tpu_custom_call" | custom-call | tf_op jit(solution)/shard_map/pallas_call | solution.py:366
  38.6 1.9 %copy.8 = bf16[4,16,16,256]{3,2,1,0:T(8,128)(2,1)} copy(bf16[4,16,16,256]{3,2,1,0:T(8,128)(2,1)} %shard_map.64) | data formatting | bytes 1048576

commit v6 on v5

--- a/solution.py
+++ b/solution.py
@@ -264,13 +264,15 @@
     for k in range(ROW - 1):
         carry = ra[k] * carry + rb[k]
         so[k + 1] = carry
-    for p in peers:
-        send(so.at[p], inc.at[r], sems_o, p, r, {"tm": base + p}).start()
+    for p in range(ROW):
+        @pl.when(p != r)
+        def _(p=p):
+            send(so.at[p], inc.at[r], sems_o, p, r, {"tm": base + p}).start()
     inc[r] = so[r]
     for k in range(ROW):
         se[k] = jnp.sum(jnp.where(at_edge[0], so[k], 0.0), axis=0, keepdims=True)
     pl.semaphore_wait(tile_ready, len(near))
-    everyone = [r] + peers
+    everyone = list(range(ROW))
 
     def to_column(p):
         return send(se.at[pl.ds(p, 1)], ie.at[pl.ds(1 + r, 1)], sems_e, p, r, {"tm": base + p, "sx": 1 - sx})

time: 40.6 us -> 40.3 us (level)
  no operation moved by 1% of the time
where the time goes in v6:
time: 40.3 us; the launch traced here: 40.1 us
  Pallas kernels  38.2 us (95%)
  local copies, waits for them, and re-layouts  1.87 us (5%)
    pallas_call x1, Pallas kernels, body(): pl.pallas_call(kernel, out_shape=jax.ShapeDtypeStruct(frames.shape, BF16)...  38.2 us
    unnamed x1, local copies, waits for them, and re-layouts  1.87 us

profile of v6, /device:TPU:57, one launch (start us, length us, event | category | flops | bytes accessed | tf_op | source)
XLA Modules:
  0.0 40.1 jit_solution(9651577897992628743)
XLA Ops:
  0.0 38.2 %shard_map.64 = bf16[4,16,16,256]{3,2,1,0:T(8,128)(2,1)} custom-call(bf16[4,16,16,256]{3,2,1,0:T(8,128)(2,1)} %refs_0_.1, bf16[25,256,128]{2,1,0:T(8,128)(2,1)} %bitcast.4, bf16[256]{0:T(256)(128)(2,1)} %refs_2_.1, f32[1,128]{1,0:T(1,128)} %bitcast.7, bf16[9,128,256]{2,1,0:T(8,128)(2,1)} %bitcast.5, f32[1,256]{1,0:T(1,128)} %bitcast.6), custom_call_target="tpu_custom_call" | custom-call | tf_op jit(solution)/shard_map/pallas_call | solution.py:368
  38.2 1.9 %copy.8 = bf16[4,16,16,256]{3,2,1,0:T(8,128)(2,1)} copy(bf16[4,16,16,256]{3,2,1,0:T(8,128)(2,1)} %shard_map.64) | data formatting | bytes 1048576

commit v7 on v6

--- a/solution.py
+++ b/solution.py
@@ -10,7 +10,7 @@
 PIX = H * W
 C, S = 256, 128
 MESH = pl.DeviceIdType.MESH
-ORDER = [8, 7, 9, 6, 10, 5, 11, 4, 12, 3, 13, 2, 14, 1, 15]
+ORDER = [8, 9, 7, 4, 12, 6, 10, 5, 11, 2, 14, 3, 13, 1, 15]
 F32 = jnp.float32
 BF16 = jnp.bfloat16
 

time: 40.3 us -> 40 us (level)
  no operation moved by 1% of the time
where the time goes in v7:
time: 40 us; the launch traced here: 39.8 us
  Pallas kernels  37.9 us (95%)
  local copies, waits for them, and re-layouts  1.87 us (5%)
    pallas_call x1, Pallas kernels, body(): pl.pallas_call(kernel, out_shape=jax.ShapeDtypeStruct(frames.shape, BF16)...  37.9 us
    unnamed x1, local copies, waits for them, and re-layouts  1.87 us

profile of v7, /device:TPU:57, one launch (start us, length us, event | category | flops | bytes accessed | tf_op | source)
XLA Modules:
  0.0 39.8 jit_solution(13291088475542825212)
XLA Ops:
  0.0 37.9 %shard_map.64 = bf16[4,16,16,256]{3,2,1,0:T(8,128)(2,1)} custom-call(bf16[4,16,16,256]{3,2,1,0:T(8,128)(2,1)} %refs_0_.1, bf16[25,256,128]{2,1,0:T(8,128)(2,1)} %bitcast.4, bf16[256]{0:T(256)(128)(2,1)} %refs_2_.1, f32[1,128]{1,0:T(1,128)} %bitcast.7, bf16[9,128,256]{2,1,0:T(8,128)(2,1)} %bitcast.5, f32[1,256]{1,0:T(1,128)} %bitcast.6), custom_call_target="tpu_custom_call" | custom-call | tf_op jit(solution)/shard_map/pallas_call | solution.py:368
  37.9 1.9 %copy.8 = bf16[4,16,16,256]{3,2,1,0:T(8,128)(2,1)} copy(bf16[4,16,16,256]{3,2,1,0:T(8,128)(2,1)} %shard_map.64) | data formatting | bytes 1048576
